TPU v7x, 768 devices: a whole 4x8x12 slice. The times are simulated.
768 devices in a mesh: rep: 16 (over y, core), grp: 48 (over x, z).
Axes of the slice: x: 4, y: 8, z: 12, core: 2. Of those that a mesh axis runs over, the one named last changes fastest.
Arguments:
- master_weight: float32 [96, 384, 2048], P('grp', 'rep'), may hold values from -0.3125 to 0.3125
- m_code: bfloat16 [96, 384, 2048], P('grp', 'rep'), may hold values from -1 to 1
- m_scale: float32 [96, 384, 16], P('grp', 'rep'), may hold values from 0.1 to 3
- v_code: bfloat16 [96, 384, 2048], P('grp', 'rep'), may hold values from 0.0099487305 to 1
- v_scale: float32 [96, 384, 16], P('grp', 'rep'), may hold values from 0.1 to 3
- placement: int32 [96], replicated, may hold values from 0 to 95, each once
- route: int32 [196608], P(('rep', 'grp')), may hold values from 0 to 95, as said below
- x_rows: bfloat16 [196608, 384], P(('rep', 'grp')), may hold values from -6 to 6
- y_cot: bfloat16 [196608, 2048], P(('rep', 'grp')), may hold values from -6 to 6
Outputs:
- y_rows: bfloat16 [196608, 2048], P(('rep', 'grp'))
- x_grad: bfloat16 [196608, 384], P(('rep', 'grp'))
- master_next: float32 [96, 384, 2048], P('grp', 'rep')
- m_code_next: bfloat16 [96, 384, 2048], P('grp', 'rep')
- m_scale_next: float32 [96, 384, 16], P('grp', 'rep')
- v_code_next: bfloat16 [96, 384, 2048], P('grp', 'rep')
- v_scale_next: float32 [96, 384, 16], P('grp', 'rep')
Inputs may be any that keep to these rules, and one draw needn't show every extreme that they name: Each expert once; slot s of the weight and moment arrays holds the expert placement[s]. `route`: in the 256 rows of one device no expert appears more than 4 times, and one expert appears exactly 4 times in the rows of every device.
All inputs are finite; a program needn't handle non-finite values. Where the computation divides by a largest or mean magnitude, that divisor is 1e-20 or more.
Results may differ from a plain program's by a relative error of at most 0.015.
Values may be sent and summed in bfloat16 or wider, within the bound.
A program may use at most 32 MiB of HBM per device.

v0:
```python
import jax
import jax.numpy as jnp
from jax import lax
from jax.sharding import PartitionSpec as P

BLOCK = 128
ADAM_STEP = 100


beta_one = 0.9
beta_two = 0.95
learn_rate = 0.01


def adam_update(master_weight, grad, m_code, m_scale, v_code, v_scale):
    full_shape = master_weight.shape
    blocked = full_shape[:-1] + (full_shape[-1] // BLOCK, BLOCK)
    m_old = (m_code.astype(jnp.float32).reshape(blocked) * m_scale[..., None]).reshape(full_shape)
    v_old = (v_code.astype(jnp.float32).reshape(blocked) * v_scale[..., None]).reshape(full_shape)
    m_next = beta_one * m_old + (1.0 - beta_one) * grad
    v_next = beta_two * v_old + (1.0 - beta_two) * grad * grad
    corr_one = 1.0 - beta_one**ADAM_STEP
    corr_two = 1.0 - beta_two**ADAM_STEP
    step_size = m_next / corr_one / (jnp.sqrt(v_next / corr_two) + 1e-08)
    master_next = master_weight - learn_rate * step_size
    m_blocks = m_next.reshape(blocked)
    v_blocks = v_next.reshape(blocked)
    m_scale_next = jnp.max(jnp.abs(m_blocks), axis=-1) + 1e-06
    v_scale_next = jnp.max(v_blocks, axis=-1) + 1e-06
    m_code_next = (m_blocks / m_scale_next[..., None]).reshape(full_shape).astype(jnp.bfloat16)
    v_code_next = (v_blocks / v_scale_next[..., None]).reshape(full_shape).astype(jnp.bfloat16)
    return (master_next, m_code_next, m_scale_next, v_code_next, v_scale_next)


def per_device(master_weight, m_code, m_scale, v_code, v_scale, placement, route, x_rows, y_cot):
    local_count, slice_rows, model_width = master_weight.shape
    row_count, hidden_width = x_rows.shape
    expert_count = placement.shape[0]
    groups = lax.axis_size("grp")
    replicas = lax.axis_size("rep")
    grad_factor = float(row_count * groups * replicas // expert_count) ** (-0.5)
    capacity = max(2, (3 * row_count + 2 * expert_count - 1) // (2 * expert_count))
    slot_rows = groups * capacity
    expert_ids = lax.iota(jnp.int32, expert_count)
    route_hot = (route[:, None] == expert_ids[None, :]).astype(jnp.int32)
    position = jnp.sum(route_hot * (jnp.cumsum(route_hot, axis=0) - 1), axis=1)
    slot = jnp.sum(jnp.where(placement[None, :] == route[:, None], expert_ids[None, :], 0), axis=1)
    target = slot % local_count * slot_rows + slot // local_count * capacity + position
    places = (target[:, None] == lax.iota(jnp.int32, local_count * slot_rows)[None, :]).astype(
        jnp.bfloat16
    )
    column_dims = (((0,), (0,)), ((), ()))
    send_x = lax.dot_general(
        places, x_rows, column_dims, preferred_element_type=jnp.float32
    ).astype(jnp.bfloat16)
    send_g = lax.dot_general(places, y_cot, column_dims, preferred_element_type=jnp.float32).astype(
        jnp.bfloat16
    )
    send_x = send_x.reshape(local_count, groups, capacity, hidden_width)
    send_g = send_g.reshape(local_count, groups, capacity, model_width)
    recv_x, recv_g = (
        lax.all_to_all(send_x, "grp", split_axis=1, concat_axis=1, tiled=True),
        lax.all_to_all(send_g, "grp", split_axis=1, concat_axis=1, tiled=True),
    )
    local_x = recv_x.reshape(local_count, slot_rows, hidden_width)
    local_g = recv_g.reshape(local_count, slot_rows, model_width)
    weight_slice = master_weight.astype(jnp.bfloat16)
    weight_rows = lax.all_gather(weight_slice, "rep", axis=1, tiled=True)
    y_total = jnp.einsum("esn,end->esd", local_x, weight_rows, preferred_element_type=jnp.float32)
    dx_part = jnp.einsum("esd,end->esn", local_g, weight_rows, preferred_element_type=jnp.float32)
    dx_total = dx_part
    y_total, dx_total = (y_total, dx_total)
    back_y = y_total.astype(jnp.bfloat16).reshape(local_count, groups, capacity, model_width)
    back_dx = dx_total.astype(jnp.bfloat16).reshape(local_count, groups, capacity, hidden_width)
    home_y, home_dx = (
        lax.all_to_all(back_y, "grp", split_axis=1, concat_axis=1, tiled=True),
        lax.all_to_all(back_dx, "grp", split_axis=1, concat_axis=1, tiled=True),
    )
    y_rows = jnp.dot(
        places, home_y.reshape(-1, model_width), preferred_element_type=jnp.float32
    ).astype(jnp.bfloat16)
    x_grad = jnp.dot(
        places, home_dx.reshape(-1, hidden_width), preferred_element_type=jnp.float32
    ).astype(jnp.bfloat16)
    grad_parts = []
    for member in range(local_count):
        outer = jnp.einsum(
            "sf,sd->fd", local_x[member], local_g[member], preferred_element_type=jnp.float32
        )
        grad_parts.append((outer * grad_factor).astype(jnp.bfloat16))
    part_grad = jnp.stack(grad_parts)
    rep_index = lax.axis_index("rep")
    slices = []
    for member in range(local_count):
        summed = lax.psum(part_grad[member], "rep").astype(jnp.float32)
        slices.append(lax.dynamic_slice_in_dim(summed, rep_index * slice_rows, slice_rows, 0))
    grad = jnp.stack(slices)
    master_next, m_code_next, m_scale_next, v_code_next, v_scale_next = adam_update(
        master_weight, grad, m_code, m_scale, v_code, v_scale
    )
    return (y_rows, x_grad, master_next, m_code_next, m_scale_next, v_code_next, v_scale_next)


def solution(mesh):
    return jax.shard_map(
        per_device,
        mesh=mesh,
        in_specs=(
            P("grp", "rep", None),
            P("grp", "rep", None),
            P("grp", "rep", None),
            P("grp", "rep", None),
            P("grp", "rep", None),
            P(),
            P(("rep", "grp")),
            P(("rep", "grp"), None),
            P(("rep", "grp"), None),
        ),
        out_specs=(
            P(("rep", "grp"), None),
            P(("rep", "grp"), None),
            P("grp", "rep", None),
            P("grp", "rep", None),
            P("grp", "rep", None),
            P("grp", "rep", None),
            P("grp", "rep", None),
        ),
        check_vma=False,
    )
```

profile of v0, /device:TPU:6, one launch (start us, length us, event | category | flops | bytes accessed | tf_op | source)
XLA Modules:
  0.0 410.3 jit_solution(16168129434543431858)
XLA Ops:
  9.7 1.3 convolution_convert_fusion.3
  11.9 18.5 %all-to-all-start = ((bf16[2,48,4,384]{3,2,0,1:T(4,128)(2,1)}), bf16[2,48,4,384]{3,2,0,1:T(4,128)(2,1)S(1)}, u32[]{:S(2)}, u32[]{:S(2)}) async-start(bf16[2,48,4,384]{3,2,0,1:T(4,128)(2,1)} %copy.49), calls=%async_computation | async-start | bytes 589824 | tf_op jit(solution)/shard_map/all_to_all | solution.py:62
  30.5 1.9 convolution_convert_fusion.1
  32.3 2.5 reshape.139
  34.8 2.2 copy.53
  37.0 10.9 %all-to-all-done = bf16[2,48,4,384]{3,2,0,1:T(4,128)(2,1)S(1)} async-done(((bf16[2,48,4,384]{3,2,0,1:T(4,128)(2,1)}), bf16[2,48,4,384]{3,2,0,1:T(4,128)(2,1)S(1)}, u32[]{:S(2)}, u32[]{:S(2)}) %all-to-all-start) | async-done | bytes 294944 | tf_op jit(solution)/shard_map/all_to_all | solution.py:62
  47.9 6.4 %all-to-all-start.2 = ((bf16[2,48,4,2048]{3,2,0,1:T(4,128)(2,1)}), bf16[2,48,4,2048]{3,2,0,1:T(4,128)(2,1)S(1)}, u32[]{:S(2)}, u32[]{:S(2)}) async-start(bf16[2,48,4,2048]{3,2,0,1:T(4,128)(2,1)} %copy.53), calls=%async_computation.2 | async-start | bytes 3145728 | tf_op jit(solution)/shard_map/all_to_all | solution.py:63
  54.5 57.4 %all-to-all-done.2 = bf16[2,48,4,2048]{3,2,0,1:T(4,128)(2,1)S(1)} async-done(((bf16[2,48,4,2048]{3,2,0,1:T(4,128)(2,1)}), bf16[2,48,4,2048]{3,2,0,1:T(4,128)(2,1)S(1)}, u32[]{:S(2)}, u32[]{:S(2)}) %all-to-all-start.2) | async-done | bytes 1572896 | tf_op jit(solution)/shard_map/all_to_all | solution.py:63
  112.6 2.2 fusion
  114.8 2.2 fusion.1
  119.9 120.9 %all-reduce.3.cloned.1.call-done = (bf16[384,2048]{1,0:T(8,128)(2,1)}, bf16[384,2048]{1,0:T(8,128)(2,1)}) async-done(((bf16[384,2048]{1,0:T(8,128)(2,1)}, bf16[384,2048]{1,0:T(8,128)(2,1)}), (bf16[384,2048]{1,0:T(8,128)(2,1)}, bf16[384,2048]{1,0:T(8,128)(2,1)})) %all-reduce.3.cloned.1.call-update) | async-done | bytes 3145744 | tf_op jit(solution)/shard_map/psum | solution.py:95
  241.7 2.0 fusion.13
  244.9 1.8 div.56
  246.7 2.7 multiply_subtract_fusion
  249.5 2.0 copy.54
  251.5 2.3 reshape.140
  253.8 42.1 %all-gather.2.cloned.1.call-done = bf16[2,384,2048]{2,1,0:T(8,128)(2,1)} async-done(((bf16[2,24,2048]{2,1,0:T(8,128)(2,1)}), bf16[2,384,2048]{2,1,0:T(8,128)(2,1)}) %all-gather.2.cloned.1.call-update) | async-done | bytes 3145744 | tf_op jit(solution)/shard_map/all_gather | solution.py:68
  295.9 3.8 convolution_convert_fusion.4
  299.7 1.0 reshape.141
  301.5 13.7 %all-to-all-start.3 = ((bf16[2,48,4,384]{3,2,0,1:T(4,128)(2,1)}), bf16[2,48,4,384]{3,2,0,1:T(4,128)(2,1)}, u32[]{:S(2)}, u32[]{:S(2)}) async-start(bf16[2,48,4,384]{3,2,0,1:T(4,128)(2,1)} %copy.55), calls=%async_computation.3 | async-start | bytes 589824 | tf_op jit(solution)/shard_map/all_to_all | solution.py:77
  315.4 2.9 convolution_convert_fusion
  318.3 2.0 reshape.137
  320.3 3.6 copy.51
  323.9 9.2 %all-to-all-done.3 = bf16[2,48,4,384]{3,2,0,1:T(4,128)(2,1)} async-done(((bf16[2,48,4,384]{3,2,0,1:T(4,128)(2,1)}), bf16[2,48,4,384]{3,2,0,1:T(4,128)(2,1)}, u32[]{:S(2)}, u32[]{:S(2)}) %all-to-all-start.3) | async-done | bytes 294944 | tf_op jit(solution)/shard_map/all_to_all | solution.py:77
  333.1 6.4 %all-to-all-start.1 = ((bf16[2,48,4,2048]{3,2,0,1:T(4,128)(2,1)}), bf16[2,48,4,2048]{3,2,0,1:T(4,128)(2,1)S(1)}, u32[]{:S(2)}, u32[]{:S(2)}) async-start(bf16[2,48,4,2048]{3,2,0,1:T(4,128)(2,1)} %copy.51), calls=%async_computation.1 | async-start | bytes 3145728 | tf_op jit(solution)/shard_map/all_to_all | solution.py:76
  342.1 1.7 divide_convert_fusion
  343.8 1.1 copy.56
  345.0 1.0 convolution_convert_fusion.5
  346.0 51.3 %all-to-all-done.1 = bf16[2,48,4,2048]{3,2,0,1:T(4,128)(2,1)S(1)} async-done(((bf16[2,48,4,2048]{3,2,0,1:T(4,128)(2,1)}), bf16[2,48,4,2048]{3,2,0,1:T(4,128)(2,1)S(1)}, u32[]{:S(2)}, u32[]{:S(2)}) %all-to-all-start.1) | async-done | bytes 1572896 | tf_op jit(solution)/shard_map/all_to_all | solution.py:76
  397.3 2.0 copy.52
  399.4 2.3 reshape.138
  401.7 1.7 convolution_convert_fusion.2
  (45 shorter events, 12.8 us)
Async XLA Ops:
  7.2 23.3 %copy-start = (bf16[256,2048]{1,0:T(8,128)(2,1)S(1)}, bf16[256,2048]{1,0:T(8,128)(2,1)}, u32[]{:S(2)}) copy-start(bf16[256,2048]{1,0:T(8,128)(2,1)} %param.17) | copy-start | bytes 3145732
  11.9 36.0 %all-to-all-start = ((bf16[2,48,4,384]{3,2,0,1:T(4,128)(2,1)}), bf16[2,48,4,384]{3,2,0,1:T(4,128)(2,1)S(1)}, u32[]{:S(2)}, u32[]{:S(2)}) async-start(bf16[2,48,4,384]{3,2,0,1:T(4,128)(2,1)} %copy.49), calls=%async_computation | async-start | bytes 589824 | tf_op jit(solution)/shard_map/all_to_all | solution.py:62
  47.9 64.0 %all-to-all-start.2 = ((bf16[2,48,4,2048]{3,2,0,1:T(4,128)(2,1)}), bf16[2,48,4,2048]{3,2,0,1:T(4,128)(2,1)S(1)}, u32[]{:S(2)}, u32[]{:S(2)}) async-start(bf16[2,48,4,2048]{3,2,0,1:T(4,128)(2,1)} %copy.53), calls=%async_computation.2 | async-start | bytes 3145728 | tf_op jit(solution)/shard_map/all_to_all | solution.py:63
  54.3 186.5 %all-reduce.3.cloned.1.call-start = ((), (), s32[]{:S(2)}) async-start(), calls=%async_computation.5 | async-start | bytes 6291456 | tf_op jit(solution)/shard_map/psum | solution.py:95
  117.1 0.7 copy-start.2
  117.1 1.8 copy-start.3
  117.1 178.8 %all-gather.2.cloned.1.call-start = ((), (), s32[]{:S(2)}) async-start(), calls=%async_computation.4 | async-start | bytes 3342336 | tf_op jit(solution)/shard_map/all_gather | solution.py:68
  241.7 3.2 copy-start.1
  301.5 31.5 %all-to-all-start.3 = ((bf16[2,48,4,384]{3,2,0,1:T(4,128)(2,1)}), bf16[2,48,4,384]{3,2,0,1:T(4,128)(2,1)}, u32[]{:S(2)}, u32[]{:S(2)}) async-start(bf16[2,48,4,384]{3,2,0,1:T(4,128)(2,1)} %copy.55), calls=%async_computation.3 | async-start | bytes 589824 | tf_op jit(solution)/shard_map/all_to_all | solution.py:77
  333.1 64.3 %all-to-all-start.1 = ((bf16[2,48,4,2048]{3,2,0,1:T(4,128)(2,1)}), bf16[2,48,4,2048]{3,2,0,1:T(4,128)(2,1)S(1)}, u32[]{:S(2)}, u32[]{:S(2)}) async-start(bf16[2,48,4,2048]{3,2,0,1:T(4,128)(2,1)} %copy.51), calls=%async_computation.1 | async-start | bytes 3145728 | tf_op jit(solution)/shard_map/all_to_all | solution.py:76
Sparse Core Ops, SparseCore 0:
  117.2 123.5 all-reduce.2
  249.6 46.2 all-gather.1
where the time goes:
time: 411 us; the launch traced here: 410 us
  waiting for transfers between devices  292 us (71%)
  starting transfers between devices  45.2 us (11%)
  local copies, waits for them, and re-layouts  32 us (8%)
  matrix products  17.1 us (4%)
  between operations  14.3 us (3%)
  other arithmetic  10 us (2%)
    psum x1, waiting for transfers between devices, per_device(): summed = lax.psum(part_grad[member], 'rep').astype(jnp.float32)  121 us
    all_to_all x1, waiting for transfers between devices, per_device(): lax.all_to_all(send_g, 'grp', split_axis=1, concat_axis=1, tiled=True)  57.4 us
    all_to_all x1, waiting for transfers between devices, per_device(): lax.all_to_all(back_y, 'grp', split_axis=1, concat_axis=1, tiled=True)  51.3 us
    all_gather x1, waiting for transfers between devices, per_device(): weight_rows = lax.all_gather(weight_slice, 'rep', axis=1, tiled=True)  42.1 us
    all_to_all x1, starting transfers between devices, per_device(): lax.all_to_all(send_x, 'grp', split_axis=1, concat_axis=1, tiled=True)  18.5 us
    all_to_all x1, starting transfers between devices, per_device(): lax.all_to_all(back_dx, 'grp', split_axis=1, concat_axis=1, tiled=True)  13.7 us
    all_to_all x1, waiting for transfers between devices, per_device(): lax.all_to_all(send_x, 'grp', split_axis=1, concat_axis=1, tiled=True)  10.9 us
    all_to_all x1, waiting for transfers between devices, per_device(): lax.all_to_all(back_dx, 'grp', split_axis=1, concat_axis=1, tiled=True)  9.16 us
  transfers between devices with their start and end apart: 6, of which 6 were waited for; matrix products, arithmetic and copies ran while one was open for 7% of the time, Pallas kernels for 0%

commit v1 on v0

v1 whole, which is shorter than its diff:
```python
import jax
import jax.numpy as jnp
from jax import lax
from jax.sharding import PartitionSpec as P

BLOCK = 128
ADAM_STEP = 100


beta_one = 0.9
beta_two = 0.95
learn_rate = 0.01


def adam_update(master_weight, grad, m_code, m_scale, v_code, v_scale):
    full_shape = master_weight.shape
    blocked = full_shape[:-1] + (full_shape[-1] // BLOCK, BLOCK)
    m_old = (m_code.astype(jnp.float32).reshape(blocked) * m_scale[..., None]).reshape(full_shape)
    v_old = (v_code.astype(jnp.float32).reshape(blocked) * v_scale[..., None]).reshape(full_shape)
    m_next = beta_one * m_old + (1.0 - beta_one) * grad
    v_next = beta_two * v_old + (1.0 - beta_two) * grad * grad
    corr_one = 1.0 - beta_one**ADAM_STEP
    corr_two = 1.0 - beta_two**ADAM_STEP
    step_size = m_next / corr_one / (jnp.sqrt(v_next / corr_two) + 1e-08)
    master_next = master_weight - learn_rate * step_size
    m_blocks = m_next.reshape(blocked)
    v_blocks = v_next.reshape(blocked)
    m_scale_next = jnp.max(jnp.abs(m_blocks), axis=-1) + 1e-06
    v_scale_next = jnp.max(v_blocks, axis=-1) + 1e-06
    m_code_next = (m_blocks / m_scale_next[..., None]).reshape(full_shape).astype(jnp.bfloat16)
    v_code_next = (v_blocks / v_scale_next[..., None]).reshape(full_shape).astype(jnp.bfloat16)
    return (master_next, m_code_next, m_scale_next, v_code_next, v_scale_next)


def per_device(master_weight, m_code, m_scale, v_code, v_scale, placement, route, x_rows, y_cot):
    local_count, slice_rows, model_width = master_weight.shape
    row_count, hidden_width = x_rows.shape
    expert_count = placement.shape[0]
    groups = lax.axis_size("grp")
    replicas = lax.axis_size("rep")
    grad_factor = float(row_count * groups * replicas // expert_count) ** (-0.5)
    capacity = max(2, (3 * row_count + 2 * expert_count - 1) // (2 * expert_count))
    block_rows = local_count * capacity
    slots = groups * block_rows
    weight_slice = lax.optimization_barrier(master_weight.astype(jnp.bfloat16))
    weight_rows = lax.all_gather(weight_slice, "rep", axis=1, tiled=True)
    expert_ids = lax.iota(jnp.int32, expert_count)
    route_hot = (route[:, None] == expert_ids[None, :]).astype(jnp.int32)
    position = jnp.sum(route_hot * (jnp.cumsum(route_hot, axis=0) - 1), axis=1)
    slot = jnp.sum(jnp.where(placement[None, :] == route[:, None], expert_ids[None, :], 0), axis=1)
    target = slot * capacity + position
    places = (target[:, None] == lax.iota(jnp.int32, slots)[None, :]).astype(jnp.bfloat16)
    rows = jnp.concatenate([x_rows, y_cot], axis=1)
    send = lax.dot_general(
        places, rows, (((0,), (0,)), ((), ())), preferred_element_type=jnp.float32
    ).astype(jnp.bfloat16)
    width = hidden_width + model_width
    recv = lax.all_to_all(
        send.reshape(groups, block_rows, width), "grp", split_axis=0, concat_axis=0, tiled=True
    ).reshape(slots, width)
    recv, weight_rows = lax.optimization_barrier((recv, weight_rows))
    member = lax.broadcasted_iota(jnp.int32, (slots, 1), 0) % block_rows // capacity
    local_x, local_g = recv[:, :hidden_width], recv[:, hidden_width:]
    wide_x = jnp.concatenate(
        [jnp.where(member == m, local_x, jnp.zeros_like(local_x)) for m in range(local_count)], axis=1
    )
    outer = lax.dot_general(
        wide_x, local_g, (((0,), (0,)), ((), ())), preferred_element_type=jnp.float32
    )
    part_grad = (outer * grad_factor).astype(jnp.bfloat16)
    part_grad = part_grad.reshape(local_count, hidden_width, model_width)
    grad = lax.psum_scatter(part_grad, "rep", scatter_dimension=1, tiled=True).astype(jnp.float32)
    weight_flat = weight_rows.reshape(local_count * hidden_width, model_width)
    y_total = jnp.dot(wide_x, weight_flat, preferred_element_type=jnp.float32)
    dx_wide = lax.dot_general(
        local_g, weight_flat, (((1,), (1,)), ((), ())), preferred_element_type=jnp.float32
    )
    dx_total = dx_wide[:, :hidden_width]
    for m in range(1, local_count):
        dx_total = jnp.where(
            member == m, dx_wide[:, m * hidden_width : (m + 1) * hidden_width], dx_total
        )
    back = jnp.concatenate([dx_total, y_total], axis=1).astype(jnp.bfloat16)
    home = lax.all_to_all(
        back.reshape(groups, block_rows, width), "grp", split_axis=0, concat_axis=0, tiled=True
    ).reshape(slots, width)
    y_rows = jnp.dot(places, home[:, hidden_width:], preferred_element_type=jnp.float32).astype(
        jnp.bfloat16
    )
    x_grad = jnp.dot(places, home[:, :hidden_width], preferred_element_type=jnp.float32).astype(
        jnp.bfloat16
    )
    return (y_rows, x_grad) + adam_update(master_weight, grad, m_code, m_scale, v_code, v_scale)


def solution(mesh):
    state = P("grp", "rep", None)
    rows = P(("rep", "grp"), None)
    return jax.shard_map(
        per_device,
        mesh=mesh,
        in_specs=(state, state, state, state, state, P(), P(("rep", "grp")), rows, rows),
        out_specs=(rows, rows, state, state, state, state, state),
        check_vma=False,
    )
```

time: 411 us -> 205 us (0.50)
  waiting for transfers between devices: 292 us -> 135 us
  local copies, waits for them, and re-layouts: 32 us -> 10.1 us
  starting transfers between devices: 45.2 us -> 24.7 us
  matrix products: 17.1 us -> 12.6 us
    psum x1 -> x0, waiting for transfers between devices: 121 us -> none  [per_device(): summed = lax.psum(part_grad[member], 'rep').astype(jnp.float32)]
    all_gather x1, waiting for transfers between devices: 42.1 us -> 0.01 us  [per_device(): weight_rows = lax.all_gather(weight_slice, 'rep', axis=1, tiled=True)]
    all_to_all x4 -> x2, starting transfers between devices: 45.1 us -> 24.6 us  [the longest x1 18.5 us: per_device(): lax.all_to_all(send.reshape(groups, block_rows, width), 'grp', split_axis...]
    reshape x12 -> x0, local copies, waits for them, and re-layouts: 17.8 us -> none  [the longest x2 5.58 us: per_device(): y_total.astype(jnp.bfloat16)]
    unnamed x14 -> x21, local copies, waits for them, and re-layouts: 2.29 us -> 9.07 us
    all_to_all x4 -> x2, waiting for transfers between devices: 129 us -> 135 us  [the longest x1 67.9 us: per_device(): lax.all_to_all(send.reshape(groups, block_rows, width), 'grp', split_axis...]
    all_to_all x4 -> x0, local copies, waits for them, and re-layouts: 5.2 us -> none  [the longest x1 2.02 us: per_device(): lax.all_to_all(back_y, 'grp', split_axis=1, concat_axis=1, tiled=True)]
    dot_general x8 -> x6, matrix products: 17.1 us -> 12.6 us  [the longest x1 3.35 us: per_device(): lax.dot_general(local_g, weight_flat, (((1,), (1,)), ((), ())), preferred...]
  transfers between devices with their start and end apart: 6 -> 4, of which waited for: 6 -> 2; matrix products, arithmetic and copies ran while one was open for 7% -> 5% of each run, Pallas kernels for 0% -> 0%
where the time goes in v1:
time: 205 us; the launch traced here: 204 us
  waiting for transfers between devices  135 us (66%)
  starting transfers between devices  24.7 us (12%)
  between operations  14.3 us (7%)
  matrix products  12.6 us (6%)
  local copies, waits for them, and re-layouts  10.1 us (5%)
  other arithmetic  7.95 us (4%)
    all_to_all x1, waiting for transfers between devices, per_device(): lax.all_to_all(send.reshape(groups, block_rows, width), 'grp', split_axis...  67.9 us
    all_to_all x1, waiting for transfers between devices, per_device(): lax.all_to_all(back.reshape(groups, block_rows, width), 'grp', split_axis...  66.6 us
    all_to_all x1, starting transfers between devices, per_device(): lax.all_to_all(send.reshape(groups, block_rows, width), 'grp', split_axis...  18.5 us
    unnamed x21, local copies, waits for them, and re-layouts  9.07 us
    all_to_all x1, starting transfers between devices, per_device(): lax.all_to_all(back.reshape(groups, block_rows, width), 'grp', split_axis...  6.03 us
  transfers between devices with their start and end apart: 4, of which 2 were waited for; matrix products, arithmetic and copies ran while one was open for 5% of the time, Pallas kernels for 0%

profile of v1, /device:TPU:6, one launch (start us, length us, event | category | flops | bytes accessed | tf_op | source)
XLA Modules:
  0.0 204.3 jit_solution(5203965449226792908)
XLA Ops:
  7.2 1.7 convert_element_type.40
  8.9 0.7 fusion.19
  9.6 0.6 reduce-window.6
  10.3 0.2 slice_reduce_fusion
  10.5 0.8 select_reduce_fusion
  11.3 3.3 %fusion = bf16[48,8,2432]{2,1,0:T(8,128)(2,1)} fusion(bf16[256,2048]{1,0:T(8,128)(2,1)} %param.17, bf16[256,384]{1,0:T(8,128)(2,1)} %param.16, s32[256]{0:T(256)S(1)} %multiply_add_fusion), kind=kOutput, calls=%fused_computation.2 | convolution fusion | flops 481673216 | bytes 3113984 | tf_op jit(solution)/shard_map/dot_general | solution.py:54
  14.6 18.5 %all-to-all-start = ((bf16[48,8,2432]{2,1,0:T(8,128)(2,1)}), bf16[48,8,2432]{2,1,0:T(8,128)(2,1)S(1)}, u32[]{:S(2)}, u32[]{:S(2)}) async-start(bf16[48,8,2432]{2,1,0:T(8,128)(2,1)} %fusion), calls=%async_computation | async-start | bytes 3735552 | tf_op jit(solution)/shard_map/all_to_all | solution.py:58
  33.2 67.9 %all-to-all-done = bf16[48,8,2432]{2,1,0:T(8,128)(2,1)S(1)} async-done(((bf16[48,8,2432]{2,1,0:T(8,128)(2,1)}), bf16[48,8,2432]{2,1,0:T(8,128)(2,1)S(1)}, u32[]{:S(2)}, u32[]{:S(2)}) %all-to-all-start) | async-done | bytes 1867808 | tf_op jit(solution)/shard_map/all_to_all | solution.py:58
  101.1 3.3 %fusion.3 = bf16[384,768]{1,0:T(8,128)(2,1)S(1)} fusion(bf16[768,2048]{1,0:T(8,128)(2,1)} %bitcast.70, bf16[384,2432]{1,0:T(8,128)(2,1)S(1)} %bitcast.59), kind=kOutput, calls=%fused_computation.8 | convolution fusion | flops 1207959552 | bytes 5308416 | tf_op jit(solution)/shard_map/dot_general | solution.py:75
  104.5 0.2 broadcast_select_fusion
  104.7 1.8 multiply_convert_fusion
  106.6 1.4 convolution_convert_fusion.1
  108.0 3.2 %copy.30 = bf16[2,384,2048]{2,0,1:T(2,128)(2,1)S(1)} copy(bf16[2,384,2048]{2,1,0:T(8,128)(2,1)S(1)} %bitcast.58) | data formatting | bytes 6291456
  111.3 3.0 %copy.33 = bf16[48,8,2,2048]{3,1,2,0:T(8,128)(2,1)} copy(bf16[48,8,2,2048]{3,2,1,0:T(2,128)(2,1)S(1)} %bitcast.56) | data formatting | bytes 6291456
  114.3 1.4 pad_maximum_fusion
  115.8 6.0 %all-to-all-start.1 = ((bf16[48,8,2432]{2,1,0:T(8,128)(2,1)}), bf16[48,8,2432]{2,1,0:T(8,128)(2,1)S(1)}, u32[]{:S(2)}, u32[]{:S(2)}) async-start(bf16[48,8,2432]{2,1,0:T(8,128)(2,1)} %pad_maximum_fusion), calls=%async_computation.1 | async-start | bytes 3735552 | tf_op jit(solution)/shard_map/all_to_all | solution.py:84
  121.8 0.1 copy.26
  121.9 0.2 mul.77
  122.2 0.2 mul.86
  122.4 66.6 %all-to-all-done.1 = bf16[48,8,2432]{2,1,0:T(8,128)(2,1)S(1)} async-done(((bf16[48,8,2432]{2,1,0:T(8,128)(2,1)}), bf16[48,8,2432]{2,1,0:T(8,128)(2,1)S(1)}, u32[]{:S(2)}, u32[]{:S(2)}) %all-to-all-start.1) | async-done | bytes 1867808 | tf_op jit(solution)/shard_map/all_to_all | solution.py:84
  189.1 1.0 convolution_convert_fusion.3
  190.1 1.7 convolution_convert_fusion.2
  191.8 1.1 reshape.144
  193.0 0.1 fusion.29
  193.2 0.2 bitcast_reduce_fusion.1
  193.4 0.7 copy.28
  194.1 0.2 div.70
  194.3 1.2 multiply_subtract_fusion
  195.6 0.2 bitcast_reduce_fusion
  195.8 0.7 copy.29
  196.4 0.2 div.73
  196.7 0.7 divide_convert_fusion
  (31 shorter events, 0.7 us)
Async XLA Ops:
  7.2 94.0 %all-gather.2.cloned.1.call-start = ((), (), s32[]{:S(2)}) async-start(), calls=%async_computation.3 | async-start | bytes 3342336 | tf_op jit(solution)/shard_map/all_gather | solution.py:46
  14.6 86.5 %all-to-all-start = ((bf16[48,8,2432]{2,1,0:T(8,128)(2,1)}), bf16[48,8,2432]{2,1,0:T(8,128)(2,1)S(1)}, u32[]{:S(2)}, u32[]{:S(2)}) async-start(bf16[48,8,2432]{2,1,0:T(8,128)(2,1)} %fusion), calls=%async_computation | async-start | bytes 3735552 | tf_op jit(solution)/shard_map/all_to_all | solution.py:58
  33.2 158.7 %reduce-scatter.4.cloned.1.call-start = ((), (), s32[]{:S(2)}) async-start(), calls=%async_computation.4 | async-start | bytes 3342336
  104.7 1.9 copy-start.5
  115.8 6.0 %copy-start.3 = (f32[2,24,16]{1,2,0:T(8,128)S(1)}, f32[2,24,16]{1,2,0:T(8,128)}, u32[]{:S(2)}) copy-start(f32[2,24,16]{1,2,0:T(8,128)} %param.11) | copy-start | bytes 9220
  115.8 6.4 %copy-start.4 = (f32[2,24,16]{1,2,0:T(8,128)S(1)}, f32[2,24,16]{1,2,0:T(8,128)}, u32[]{:S(2)}) copy-start(f32[2,24,16]{1,2,0:T(8,128)} %param.13) | copy-start | bytes 9220
  115.8 73.3 %all-to-all-start.1 = ((bf16[48,8,2432]{2,1,0:T(8,128)(2,1)}), bf16[48,8,2432]{2,1,0:T(8,128)(2,1)S(1)}, u32[]{:S(2)}, u32[]{:S(2)}) async-start(bf16[48,8,2432]{2,1,0:T(8,128)(2,1)} %pad_maximum_fusion), calls=%async_computation.1 | async-start | bytes 3735552 | tf_op jit(solution)/shard_map/all_to_all | solution.py:84
  189.1 3.9 %copy-start.1 = (bf16[2,24,2048]{2,1,0:T(8,128)(2,1)S(1)}, bf16[2,24,2048]{2,1,0:T(8,128)(2,1)}, u32[]{:S(2)}) copy-start(bf16[2,24,2048]{2,1,0:T(8,128)(2,1)} %param.10) | copy-start | bytes 589828
  192.9 1.4 copy-start
  192.9 1.4 copy-start.2
Sparse Core Ops, SparseCore 0:
  11.0 52.4 all-gather.1
  114.5 61.8 reduce-scatter.3

commit v2 on v1

v2 whole, which is shorter than its diff:
```python
import jax
import jax.numpy as jnp
from jax import lax
from jax.experimental import pallas as pl
from jax.experimental.pallas import tpu as pltpu
from jax.sharding import PartitionSpec as P

BLOCK = 128
ADAM_STEP = 100
GRID_X = 4
GRID_Y = 8
GRID_Z = 12
HALF_Z = GRID_Z // 2
PEERS = 2 * GRID_X * HALF_Z
MESH = pl.DeviceIdType.MESH
TIE = 3
VMEM_LIMIT = 40 * 1024 * 1024


beta_one = 0.9
beta_two = 0.95
learn_rate = 0.01


def adam_update(master_weight, grad, m_code, m_scale, v_code, v_scale):
    full_shape = master_weight.shape
    blocked = full_shape[:-1] + (full_shape[-1] // BLOCK, BLOCK)
    m_old = (m_code.astype(jnp.float32).reshape(blocked) * m_scale[..., None]).reshape(full_shape)
    v_old = (v_code.astype(jnp.float32).reshape(blocked) * v_scale[..., None]).reshape(full_shape)
    m_next = beta_one * m_old + (1.0 - beta_one) * grad
    v_next = beta_two * v_old + (1.0 - beta_two) * grad * grad
    corr_one = 1.0 - beta_one**ADAM_STEP
    corr_two = 1.0 - beta_two**ADAM_STEP
    step_size = m_next / corr_one / (jnp.sqrt(v_next / corr_two) + 1e-08)
    master_next = master_weight - learn_rate * step_size
    m_blocks = m_next.reshape(blocked)
    v_blocks = v_next.reshape(blocked)
    m_scale_next = jnp.max(jnp.abs(m_blocks), axis=-1) + 1e-06
    v_scale_next = jnp.max(v_blocks, axis=-1) + 1e-06
    m_code_next = (m_blocks / m_scale_next[..., None]).reshape(full_shape).astype(jnp.bfloat16)
    v_code_next = (v_blocks / v_scale_next[..., None]).reshape(full_shape).astype(jnp.bfloat16)
    return (master_next, m_code_next, m_scale_next, v_code_next, v_scale_next)


def offset_of(d):
    return jnp.where(d < TIE, d, d - HALF_Z)


class Place:
    def __init__(self):
        rep, grp = lax.axis_index("rep"), lax.axis_index("grp")
        self.y, self.c = rep // 2, rep % 2
        self.x, self.z = grp // GRID_Z, grp % GRID_Z

    def device(self, y=0, c=0, x=0, z=0):
        rep = (self.y + y + GRID_Y) % GRID_Y * 2 + (self.c + c) % 2
        grp = (self.x + x) % GRID_X * GRID_Z + (self.z + z + GRID_Z) % GRID_Z
        return rep, grp

    def slot(self, c, x, d):
        return ((self.c + c) % 2 * GRID_X + (self.x + x) % GRID_X) * HALF_Z + d


def signal(device):
    pl.semaphore_signal(
        pltpu.get_barrier_semaphore(), inc=1, device_id=device, device_id_type=MESH
    )


def enter(place, sign):
    def greet(i, carry):
        d, c, x = i // (2 * GRID_X), i // GRID_X % 2, i % GRID_X

        @pl.when(i != 0)
        def _():
            signal(place.device(c=c, x=x, z=-sign * offset_of(d)))

        return carry

    signal(place.device(z=HALF_Z))
    signal(place.device(c=1, z=HALF_Z))
    signal(place.device(y=1))
    signal(place.device(y=-1))
    lax.fori_loop(0, PEERS, greet, 0)
    pl.semaphore_wait(pltpu.get_barrier_semaphore(), PEERS - 1 + 4)


def row_copy(place, source, target, send_sem, recv_sem, sign, c, x, d):
    there = place.slot(c, x, d)
    here = place.slot(0, 0, d)
    return pltpu.make_async_remote_copy(
        src_ref=source.at[there],
        dst_ref=target.at[here],
        send_sem=send_sem.at[there],
        recv_sem=recv_sem.at[here],
        device_id=place.device(c=c, x=x, z=sign * offset_of(d)),
        device_id_type=MESH,
    )


def rows_start(place, source, target, send_sem, recv_sem, sign):
    own = place.slot(0, 0, 0)
    pltpu.make_async_copy(source.at[own], target.at[own], recv_sem.at[own]).start()

    def step(i, carry):
        d, c, x = i // (2 * GRID_X), i // GRID_X % 2, i % GRID_X
        d = (d + 3) % HALF_Z

        @pl.when(jnp.logical_or(d != 0, i % (2 * GRID_X) != 0))
        def _():
            row_copy(place, source, target, send_sem, recv_sem, sign, c, x, d).start()

        return carry

    lax.fori_loop(0, PEERS, step, 0)


def rows_wait(place, source, target, send_sem, recv_sem, sign):
    own = place.slot(0, 0, 0)

    def step(i, carry):
        copy = pltpu.make_async_remote_copy(
            src_ref=source.at[i],
            dst_ref=target.at[i],
            send_sem=send_sem.at[i],
            recv_sem=recv_sem.at[i],
            device_id=place.device(y=1),
            device_id_type=MESH,
        )

        @pl.when(i != own)
        def _():
            copy.wait_send()
            copy.wait_recv()

        return carry

    lax.fori_loop(0, PEERS, step, 0)
    pltpu.make_async_copy(source.at[own], target.at[own], recv_sem.at[own]).wait()


def remote(source, target, send_sem, recv_sem, device):
    return pltpu.make_async_remote_copy(
        src_ref=source,
        dst_ref=target,
        send_sem=send_sem,
        recv_sem=recv_sem,
        device_id=device,
        device_id_type=MESH,
    )


def dispatch_kernel(
    rows_ref, slice_ref, recv_ref, full_ref,
    row_send, row_recv, first_send, first_recv, ring_send, ring_recv, local_sem,
):
    place = Place()
    y, c = place.y, place.c
    enter(place, 1)
    own = pltpu.make_async_copy(slice_ref.at[c], full_ref.at[0, y, c], local_sem)
    own.start()
    far = []
    for m in range(2):
        far.append(
            remote(
                slice_ref.at[(c + m) % 2], full_ref.at[1, y, c],
                first_send.at[1 + m], first_recv.at[1 + c], place.device(c=m, z=HALF_Z),
            )
        )
        far[m].start()
    near = remote(
        slice_ref.at[1 - c], full_ref.at[0, y, c],
        first_send.at[0], first_recv.at[0], place.device(c=1),
    )
    near.start()
    rows_start(place, rows_ref, recv_ref, row_send, row_recv, 1)
    pending = []
    for h in range(2):
        if h == 0:
            own.wait()
            near.wait()
        else:
            for m in range(2):
                remote(
                    slice_ref.at[m], full_ref.at[1, y, m],
                    first_send.at[1 + m], first_recv.at[1 + m], place.device(z=HALF_Z),
                ).wait()
        for step in range(4):
            arrived = []
            for way in range(2):
                sign = 1 - 2 * way
                origin = (y - sign * step + GRID_Y) % GRID_Y
                if step < 3:
                    block = full_ref.at[h, origin]
                else:
                    block = full_ref.at[h, origin, way]
                copy = remote(
                    block, block, ring_send.at[h, way, step], ring_recv.at[h, way, step],
                    place.device(y=sign),
                )
                copy.start()
                pending.append(copy)
                origin = (y - sign * (step + 1) + GRID_Y) % GRID_Y
                if step < 3:
                    block = full_ref.at[h, origin]
                else:
                    block = full_ref.at[h, origin, way]
                arrived.append(
                    remote(
                        block, block, ring_send.at[h, way, step], ring_recv.at[h, way, step],
                        place.device(y=sign),
                    )
                )
            for copy in arrived:
                copy.wait_recv()
    for copy in pending:
        copy.wait_send()
    rows_wait(place, rows_ref, recv_ref, row_send, row_recv, 1)


def return_kernel(
    rows_ref, part_ref, home_ref, grad_ref,
    hold, total, row_send, row_recv, ring_send, ring_recv, last_send, last_recv, local_sem,
):
    place = Place()
    y, c = place.y, place.c
    enter(place, -1)
    rows_start(place, rows_ref, home_ref, row_send, row_recv, -1)
    pending = []
    for h in (1, 0):
        for step in range(4):
            arrived = []
            for way in range(2):
                sign = 1 - 2 * way
                target = (y + sign * (4 - step) + GRID_Y) % GRID_Y
                if step == 0:
                    source, into = part_ref.at[h, target, way], hold.at[h, way, step, way]
                else:
                    held = hold.at[h, way, step - 1]
                    if step == 1:
                        held[way] = (
                            held[way].astype(jnp.float32)
                            + part_ref[h, target, way].astype(jnp.float32)
                        ).astype(jnp.bfloat16)
                        held[1 - way] = part_ref[h, target, 1 - way]
                    else:
                        held[...] = (
                            held[...].astype(jnp.float32)
                            + part_ref[h, target].astype(jnp.float32)
                        ).astype(jnp.bfloat16)
                    source, into = held, hold.at[h, way, step]
                copy = remote(
                    source, into, ring_send.at[h, way, step], ring_recv.at[h, way, step],
                    place.device(y=sign),
                )
                copy.start()
                pending.append(copy)
                arrived.append(copy)
            for copy in arrived:
                copy.wait_recv()
        total[h] = (
            part_ref[h, y].astype(jnp.float32)
            + hold[h, 0, 3].astype(jnp.float32)
            + hold[h, 1, 3].astype(jnp.float32)
        ).astype(jnp.bfloat16)
        if h == 1:
            far = []
            for m in range(2):
                far.append(
                    remote(
                        total.at[1, (c + m) % 2], grad_ref.at[c, 1],
                        last_send.at[1 + m], last_recv.at[1 + c], place.device(c=m, z=HALF_Z),
                    )
                )
                far[m].start()
        else:
            own = pltpu.make_async_copy(total.at[0, c], grad_ref.at[c, 0], local_sem)
            own.start()
            near = remote(
                total.at[0, 1 - c], grad_ref.at[c, 0],
                last_send.at[0], last_recv.at[0], place.device(c=1),
            )
            near.start()
    for copy in pending:
        copy.wait_send()
    own.wait()
    near.wait()
    for m in range(2):
        remote(
            total.at[1, m], grad_ref.at[m, 1],
            last_send.at[1 + m], last_recv.at[1 + m], place.device(z=HALF_Z),
        ).wait()
    rows_wait(place, rows_ref, home_ref, row_send, row_recv, -1)


VMEM = pl.BlockSpec(memory_space=pltpu.VMEM)
DMA = pltpu.SemaphoreType.DMA


def dispatch(rows, weight_slice):
    members, slice_rows, width = weight_slice.shape
    return pl.pallas_call(
        dispatch_kernel,
        out_shape=(
            jax.ShapeDtypeStruct(rows.shape, rows.dtype),
            jax.ShapeDtypeStruct((2, GRID_Y, 2, slice_rows, width), weight_slice.dtype),
        ),
        in_specs=[VMEM] * 2,
        out_specs=(VMEM, VMEM),
        scratch_shapes=[
            DMA((PEERS,)), DMA((PEERS,)), DMA((3,)), DMA((3,)),
            DMA((2, 2, 4)), DMA((2, 2, 4)), DMA(()),
        ],
        compiler_params=pltpu.CompilerParams(
            collective_id=0, has_side_effects=True, vmem_limit_bytes=VMEM_LIMIT
        ),
        name="dispatch",
    )(rows, weight_slice)


def give_back(rows, part):
    slice_rows, width = part.shape[-2:]
    return pl.pallas_call(
        return_kernel,
        out_shape=(
            jax.ShapeDtypeStruct(rows.shape, rows.dtype),
            jax.ShapeDtypeStruct((2, 2, slice_rows, width), part.dtype),
        ),
        in_specs=[VMEM] * 2,
        out_specs=(VMEM, VMEM),
        scratch_shapes=[
            pltpu.VMEM((2, 2, 4, 2, slice_rows, width), part.dtype),
            pltpu.VMEM((2, 2, slice_rows, width), part.dtype),
            DMA((PEERS,)), DMA((PEERS,)), DMA((2, 2, 4)), DMA((2, 2, 4)),
            DMA((3,)), DMA((3,)), DMA(()),
        ],
        compiler_params=pltpu.CompilerParams(
            collective_id=1, has_side_effects=True, vmem_limit_bytes=VMEM_LIMIT
        ),
        name="give_back",
    )(rows, part)


def per_device(master_weight, m_code, m_scale, v_code, v_scale, placement, route, x_rows, y_cot):
    members, slice_rows, model_width = master_weight.shape
    row_count, hidden_width = x_rows.shape
    expert_count = placement.shape[0]
    groups = lax.axis_size("grp")
    replicas = lax.axis_size("rep")
    grad_factor = float(row_count * groups * replicas // expert_count) ** (-0.5)
    capacity = max(2, (3 * row_count + 2 * expert_count - 1) // (2 * expert_count))
    block_rows = 2 * capacity
    slots = PEERS * block_rows
    weight_slice = master_weight.astype(jnp.bfloat16)
    expert_ids = lax.iota(jnp.int32, expert_count)
    route_hot = (route[:, None] == expert_ids[None, :]).astype(jnp.int32)
    position = jnp.sum(route_hot * (jnp.cumsum(route_hot, axis=0) - 1), axis=1)
    slot = jnp.sum(jnp.where(placement[None, :] == route[:, None], expert_ids[None, :], 0), axis=1)
    here_z = lax.axis_index("grp") % GRID_Z
    core, chip_x, chip_z = slot % members, slot // members // GRID_Z, slot // members % GRID_Z
    d = (chip_z - here_z + GRID_Z) % HALF_Z
    far = ((here_z + offset_of(d) + GRID_Z) % GRID_Z != chip_z).astype(jnp.int32)
    target = ((core * GRID_X + chip_x) * HALF_Z + d) * block_rows + far * capacity + position
    places = (target[:, None] == lax.iota(jnp.int32, slots)[None, :]).astype(jnp.bfloat16)
    rows = jnp.concatenate([x_rows, y_cot], axis=1)
    send = lax.dot_general(
        places, rows, (((0,), (0,)), ((), ())), preferred_element_type=jnp.float32
    ).astype(jnp.bfloat16)
    width = hidden_width + model_width
    recv, full = dispatch(send.reshape(PEERS, block_rows, width), weight_slice)
    recv = recv.reshape(slots, width)
    half = lax.broadcasted_iota(jnp.int32, (slots, 1), 0) % block_rows // capacity
    local_x, local_g = recv[:, :hidden_width], recv[:, hidden_width:]
    wide_x = jnp.concatenate(
        [jnp.where(half == h, local_x, jnp.zeros_like(local_x)) for h in range(2)], axis=1
    )
    outer = lax.dot_general(
        wide_x, local_g, (((0,), (0,)), ((), ())), preferred_element_type=jnp.float32
    )
    part = (outer * grad_factor).astype(jnp.bfloat16)
    part = part.reshape(2, GRID_Y, 2, slice_rows, model_width)
    weight_flat = full.reshape(2 * hidden_width, model_width)
    y_total = jnp.dot(wide_x, weight_flat, preferred_element_type=jnp.float32)
    dx_wide = lax.dot_general(
        local_g, weight_flat, (((1,), (1,)), ((), ())), preferred_element_type=jnp.float32
    )
    dx_total = jnp.where(half == 0, dx_wide[:, :hidden_width], dx_wide[:, hidden_width:])
    back = jnp.concatenate([dx_total, y_total], axis=1).astype(jnp.bfloat16)
    home, grad_pairs = give_back(back.reshape(PEERS, block_rows, width), part)
    home = home.reshape(slots, width)
    y_rows = jnp.dot(places, home[:, hidden_width:], preferred_element_type=jnp.float32).astype(
        jnp.bfloat16
    )
    x_grad = jnp.dot(places, home[:, :hidden_width], preferred_element_type=jnp.float32).astype(
        jnp.bfloat16
    )
    grad = jnp.sum(grad_pairs.astype(jnp.float32), axis=1)
    return (y_rows, x_grad) + adam_update(master_weight, grad, m_code, m_scale, v_code, v_scale)


def solution(mesh):
    state = P("grp", "rep", None)
    rows = P(("rep", "grp"), None)
    return jax.shard_map(
        per_device,
        mesh=mesh,
        in_specs=(state, state, state, state, state, P(), P(("rep", "grp")), rows, rows),
        out_specs=(rows, rows, state, state, state, state, state),
        check_vma=False,
    )
```

time: 205 us -> 158 us (0.77)
  the two profiles are of different devices: /device:TPU:6 before, /device:TPU:1 now
where the time goes in v2:
time: 158 us; the launch traced here: 157 us
  Pallas kernels  139 us (88%)
  matrix products  9.42 us (6%)
  other arithmetic  5.03 us (3%)
  local copies, waits for them, and re-layouts  2.94 us (2%)
    pallas_call x1, Pallas kernels, dispatch(): pl.pallas_call(dispatch_kernel, out_shape=(jax.ShapeDtypeStruct(rows.shap...  75.1 us
    pallas_call x1, Pallas kernels, give_back(): pl.pallas_call(return_kernel, out_shape=(jax.ShapeDtypeStruct(rows.shape,...  64.1 us

profile of v2, /device:TPU:1, one launch (start us, length us, event | category | flops | bytes accessed | tf_op | source)
XLA Modules:
  0.0 157.5 jit_solution(9958441607752707875)
XLA Ops:
  0.6 0.7 fusion.18
  1.4 0.6 reduce-window.6
  2.0 0.2 slice_reduce_fusion
  2.3 0.8 select_reduce_fusion
  3.1 2.0 %fusion.rows_ref = bf16[48,8,2432]{2,1,0:T(8,128)(2,1)S(1)} fusion(bf16[256,2048]{1,0:T(8,128)(2,1)} %param.17, bf16[256,384]{1,0:T(8,128)(2,1)} %param.16, s32[256]{0:T(256)S(1)} %fusion.31), kind=kOutput, calls=%fused_computation.2 | convolution fusion | flops 481673216 | bytes 3113984 | tf_op jit(solution)/shard_map/dot_general | solution.py:366
  5.2 75.1 %dispatch.1 = (bf16[48,8,2432]{2,1,0:T(8,128)(2,1)S(1)}, bf16[2,8,2,24,2048]{4,3,2,1,0:T(8,128)(2,1)S(1)}) custom-call(bf16[48,8,2432]{2,1,0:T(8,128)(2,1)S(1)} %fusion.rows_ref, bf16[2,24,2048]{2,1,0:T(8,128)(2,1)S(1)} %convert_element_type.41.slice_ref), custom_call_target="tpu_custom_call" | custom-call | tf_op jit(solution)/shard_map/dispatch/pallas_call | solution.py:302
  80.3 1.4 fusion.3
  81.7 0.2 broadcast_select_fusion.1
  82.0 1.4 convolution_convert_fusion.1
  83.3 0.2 pad_maximum_fusion.rows_ref
  83.5 1.8 %multiply_convert_fusion = bf16[768,2048]{1,0:T(8,128)(2,1)S(1)} fusion(bf16[384,2432]{1,0:T(8,128)(2,1)S(1)} %bitcast.54, bf16[384,384]{1,0:T(8,128)(2,1)S(1)} %get-tuple-element.29, bf16[384,384]{1,0:T(8,128)(2,1)S(1)} %get-tuple-element.28), kind=kOutput, calls=%fused_computation | convolution fusion | flops 1212284928 | bytes 5308416 | tf_op jit(solution)/shard_map/dot_general | solution.py:377
  85.3 64.1 %give_back.1 = (bf16[48,8,2432]{2,1,0:T(8,128)(2,1)S(1)}, bf16[2,2,24,2048]{3,2,1,0:T(8,128)(2,1)S(1)}) custom-call(bf16[48,8,2432]{2,1,0:T(8,128)(2,1)S(1)} %pad_maximum_fusion.rows_ref, bf16[2,8,2,24,2048]{4,3,2,1,0:T(8,128)(2,1)S(1)} %bitcast.51), custom_call_target="tpu_custom_call" | custom-call | tf_op jit(solution)/shard_map/give_back/pallas_call | solution.py:323
  149.5 1.7 %convolution_convert_fusion.2 = bf16[256,2048]{1,0:T(8,128)(2,1)} fusion(bf16[384,2432]{1,0:T(8,128)(2,1)S(1)} %bitcast.57, s32[256]{0:T(256)S(1)} %fusion.31), kind=kOutput, calls=%fused_computation.4 | convolution fusion | flops 403275776 | bytes 2622464 | tf_op jit(solution)/shard_map/dot_general | solution.py:391
  151.2 1.0 convolution_convert_fusion.3
  152.3 0.1 copy.26
  152.4 0.2 mul.99
  152.5 0.1 mul.100
  152.6 0.1 fusion.35
  152.7 0.2 copy-done.4
  152.9 0.1 copy.27
  153.0 0.2 mul.106
  153.2 0.1 copy.31
  153.3 0.2 bitcast_reduce_fusion.1
  153.5 0.2 div.94
  153.8 1.1 multiply_subtract_fusion
  154.9 0.7 copy.28
  155.6 0.1 copy.32
  155.6 0.2 bitcast_reduce_fusion
  155.8 0.2 div.97
  156.0 0.1 div.98
  156.1 0.7 divide_convert_fusion
  156.8 0.7 copy.29
  (19 shorter events, 0.3 us)
Async XLA Ops:
  0.6 4.6 %copy-start = (f32[2,24,2048]{2,1,0:T(8,128)S(1)}, f32[2,24,2048]{2,1,0:T(8,128)}, u32[]{:S(2)}) copy-start(f32[2,24,2048]{2,1,0:T(8,128)} %param.9) | copy-start | bytes 1179652
  149.4 2.8 %copy-start.3 = (f32[2,24,16]{1,2,0:T(8,128)S(1)}, f32[2,24,16]{1,2,0:T(8,128)}, u32[]{:S(2)}) copy-start(f32[2,24,16]{1,2,0:T(8,128)} %param.11) | copy-start | bytes 9220
  151.2 1.4 copy-start.1
  152.2 0.7 copy-start.4
  152.7 1.0 copy-start.2

commit v3 on v2

--- a/solution.py
+++ b/solution.py
@@ -13,7 +13,9 @@
 HALF_Z = GRID_Z // 2
 PEERS = 2 * GRID_X * HALF_Z
 MESH = pl.DeviceIdType.MESH
-TIE = 3
+HOPS = 4
+FIRST_ROWS = 4
+FIRST_BACK = 24
 VMEM_LIMIT = 40 * 1024 * 1024
 
 
@@ -42,8 +44,8 @@
     return (master_next, m_code_next, m_scale_next, v_code_next, v_scale_next)
 
 
-def offset_of(d):
-    return jnp.where(d < TIE, d, d - HALF_Z)
+def offset_of(d, member):
+    return jnp.where(d < 4 - member, d, d - HALF_Z)
 
 
 class Place:
@@ -67,52 +69,52 @@
     )
 
 
+def peer(i):
+    k, c, x = i // (2 * GRID_X), i // GRID_X % 2, i % GRID_X
+    d = (3 + jnp.where(k % 2 == 1, (k + 1) // 2, -(k // 2))) % HALF_Z
+    return c, x, d
+
+
 def enter(place, sign):
     def greet(i, carry):
-        d, c, x = i // (2 * GRID_X), i // GRID_X % 2, i % GRID_X
-
-        @pl.when(i != 0)
+        c, x, d = peer(i)
+        member = place.c if sign == 1 else (place.c + c) % 2
+
+        @pl.when(jnp.logical_or(d != 0, i % (2 * GRID_X) != 0))
         def _():
-            signal(place.device(c=c, x=x, z=-sign * offset_of(d)))
+            signal(place.device(c=c, x=x, z=-sign * offset_of(d, member)))
 
         return carry
 
-    signal(place.device(z=HALF_Z))
-    signal(place.device(c=1, z=HALF_Z))
+    signal(place.device(z=HALF_Z // 2))
+    signal(place.device(z=-(HALF_Z // 2)))
+    signal(place.device(c=1, z=HALF_Z // 2))
     signal(place.device(y=1))
     signal(place.device(y=-1))
     lax.fori_loop(0, PEERS, greet, 0)
-    pl.semaphore_wait(pltpu.get_barrier_semaphore(), PEERS - 1 + 4)
-
-
-def row_copy(place, source, target, send_sem, recv_sem, sign, c, x, d):
-    there = place.slot(c, x, d)
-    here = place.slot(0, 0, d)
-    return pltpu.make_async_remote_copy(
-        src_ref=source.at[there],
-        dst_ref=target.at[here],
-        send_sem=send_sem.at[there],
-        recv_sem=recv_sem.at[here],
-        device_id=place.device(c=c, x=x, z=sign * offset_of(d)),
-        device_id_type=MESH,
-    )
-
-
-def rows_start(place, source, target, send_sem, recv_sem, sign):
+    pl.semaphore_wait(pltpu.get_barrier_semaphore(), PEERS - 1 + 5)
+
+
+def rows_start(place, source, target, send_sem, recv_sem, sign, low, high):
     own = place.slot(0, 0, 0)
-    pltpu.make_async_copy(source.at[own], target.at[own], recv_sem.at[own]).start()
+    if low == 0:
+        pltpu.make_async_copy(source.at[own], target.at[own], recv_sem.at[own]).start()
 
     def step(i, carry):
-        d, c, x = i // (2 * GRID_X), i // GRID_X % 2, i % GRID_X
-        d = (d + 3) % HALF_Z
+        c, x, d = peer(i)
+        member = (place.c + c) % 2 if sign == 1 else place.c
+        there, here = place.slot(c, x, d), place.slot(0, 0, d)
 
         @pl.when(jnp.logical_or(d != 0, i % (2 * GRID_X) != 0))
         def _():
-            row_copy(place, source, target, send_sem, recv_sem, sign, c, x, d).start()
+            remote(
+                source.at[there], target.at[here], send_sem.at[there], recv_sem.at[here],
+                place.device(c=c, x=x, z=sign * offset_of(d, member)),
+            ).start()
 
         return carry
 
-    lax.fori_loop(0, PEERS, step, 0)
+    lax.fori_loop(low, high, step, 0)
 
 
 def rows_wait(place, source, target, send_sem, recv_sem, sign):
@@ -150,146 +152,169 @@
     )
 
 
+def far_start(place, first, second, relay, send_sem, recv_sem):
+    up = remote(
+        first, relay.at[0], send_sem.at[0], recv_sem.at[0], place.device(z=HALF_Z // 2)
+    )
+    down = remote(
+        second, relay.at[1], send_sem.at[1], recv_sem.at[1],
+        place.device(c=1, z=-(HALF_Z // 2)),
+    )
+    up.start()
+    down.start()
+    return [up, down]
+
+
+def far_relay(place, legs, relay, target_up, target_down, send_sem, recv_sem):
+    up = remote(
+        relay.at[0], target_up, send_sem.at[2], recv_sem.at[2], place.device(z=HALF_Z // 2)
+    )
+    down = remote(
+        relay.at[1], target_down, send_sem.at[3], recv_sem.at[3],
+        place.device(z=-(HALF_Z // 2)),
+    )
+    for leg, copy in zip(legs, (up, down)):
+        leg.wait_recv()
+        copy.start()
+    return [up, down]
+
+
+def ring_copy(place, source, target, send_sem, recv_sem, h, half, way, step):
+    return remote(
+        source, target, send_sem.at[h, half, way, step], recv_sem.at[h, half, way, step],
+        place.device(y=1 - 2 * way),
+    )
+
+
 def dispatch_kernel(
     rows_ref, slice_ref, recv_ref, full_ref,
-    row_send, row_recv, first_send, first_recv, ring_send, ring_recv, local_sem,
+    relay, row_send, row_recv, far_send, far_recv, near_send, near_recv,
+    ring_send, ring_recv, local_sem,
 ):
     place = Place()
     y, c = place.y, place.c
     enter(place, 1)
     own = pltpu.make_async_copy(slice_ref.at[c], full_ref.at[0, y, c], local_sem)
     own.start()
-    far = []
-    for m in range(2):
-        far.append(
-            remote(
-                slice_ref.at[(c + m) % 2], full_ref.at[1, y, c],
-                first_send.at[1 + m], first_recv.at[1 + c], place.device(c=m, z=HALF_Z),
-            )
-        )
-        far[m].start()
     near = remote(
-        slice_ref.at[1 - c], full_ref.at[0, y, c],
-        first_send.at[0], first_recv.at[0], place.device(c=1),
+        slice_ref.at[1 - c], full_ref.at[0, y, c], near_send, near_recv, place.device(c=1)
     )
     near.start()
-    rows_start(place, rows_ref, recv_ref, row_send, row_recv, 1)
-    pending = []
-    for h in range(2):
-        if h == 0:
-            own.wait()
-            near.wait()
-        else:
-            for m in range(2):
-                remote(
-                    slice_ref.at[m], full_ref.at[1, y, m],
-                    first_send.at[1 + m], first_recv.at[1 + m], place.device(z=HALF_Z),
-                ).wait()
-        for step in range(4):
-            arrived = []
+    legs = far_start(place, slice_ref.at[c], slice_ref.at[1 - c], relay, far_send, far_recv)
+    rows_start(place, rows_ref, recv_ref, row_send, row_recv, 1, 0, FIRST_ROWS)
+    sent = []
+
+    def ring(h, step):
+        for half in range(2):
             for way in range(2):
-                sign = 1 - 2 * way
-                origin = (y - sign * step + GRID_Y) % GRID_Y
-                if step < 3:
-                    block = full_ref.at[h, origin]
-                else:
-                    block = full_ref.at[h, origin, way]
-                copy = remote(
-                    block, block, ring_send.at[h, way, step], ring_recv.at[h, way, step],
-                    place.device(y=sign),
-                )
+                if step >= HOPS - (half != way):
+                    continue
+                if step > 0:
+                    sent[index[h, half, way]].wait_recv()
+                origin = (y - (1 - 2 * way) * step + GRID_Y) % GRID_Y
+                block = full_ref.at[h, origin, half]
+                copy = ring_copy(place, block, block, ring_send, ring_recv, h, half, way, step)
                 copy.start()
-                pending.append(copy)
-                origin = (y - sign * (step + 1) + GRID_Y) % GRID_Y
-                if step < 3:
-                    block = full_ref.at[h, origin]
-                else:
-                    block = full_ref.at[h, origin, way]
-                arrived.append(
-                    remote(
-                        block, block, ring_send.at[h, way, step], ring_recv.at[h, way, step],
-                        place.device(y=sign),
-                    )
-                )
-            for copy in arrived:
-                copy.wait_recv()
-    for copy in pending:
+                index[h, half, way] = len(sent)
+                sent.append(copy)
+
+    index = {}
+    own.wait()
+    near.wait()
+    ring(0, 0)
+    ring(0, 1)
+    more = far_relay(
+        place, legs, relay, full_ref.at[1, y, c], full_ref.at[1, y, 1 - c], far_send, far_recv
+    )
+    rows_start(place, rows_ref, recv_ref, row_send, row_recv, 1, FIRST_ROWS, PEERS)
+    ring(0, 2)
+    for copy in more:
+        copy.wait_recv()
+    ring(1, 0)
+    ring(0, 3)
+    ring(1, 1)
+    ring(1, 2)
+    ring(1, 3)
+    for i in index.values():
+        sent[i].wait_recv()
+    for copy in legs + more + sent:
         copy.wait_send()
     rows_wait(place, rows_ref, recv_ref, row_send, row_recv, 1)
 
 
 def return_kernel(
     rows_ref, part_ref, home_ref, grad_ref,
-    hold, total, row_send, row_recv, ring_send, ring_recv, last_send, last_recv, local_sem,
+    relay, hold, total, row_send, row_recv, far_send, far_recv, near_send, near_recv,
+    ring_send, ring_recv, local_sem,
 ):
     place = Place()
     y, c = place.y, place.c
     enter(place, -1)
-    rows_start(place, rows_ref, home_ref, row_send, row_recv, -1)
-    pending = []
-    for h in (1, 0):
-        for step in range(4):
-            arrived = []
+    rows_start(place, rows_ref, home_ref, row_send, row_recv, -1, 0, FIRST_BACK)
+    sent = []
+    index = {}
+
+    def ring(h, step):
+        for half in range(2):
             for way in range(2):
-                sign = 1 - 2 * way
-                target = (y + sign * (4 - step) + GRID_Y) % GRID_Y
-                if step == 0:
-                    source, into = part_ref.at[h, target, way], hold.at[h, way, step, way]
+                first = int(half != way)
+                if step < first:
+                    continue
+                target = (y + (1 - 2 * way) * (HOPS - step) + GRID_Y) % GRID_Y
+                if step == first:
+                    source = part_ref.at[h, target, half]
                 else:
-                    held = hold.at[h, way, step - 1]
-                    if step == 1:
-                        held[way] = (
-                            held[way].astype(jnp.float32)
-                            + part_ref[h, target, way].astype(jnp.float32)
-                        ).astype(jnp.bfloat16)
-                        held[1 - way] = part_ref[h, target, 1 - way]
-                    else:
-                        held[...] = (
-                            held[...].astype(jnp.float32)
-                            + part_ref[h, target].astype(jnp.float32)
-                        ).astype(jnp.bfloat16)
-                    source, into = held, hold.at[h, way, step]
-                copy = remote(
-                    source, into, ring_send.at[h, way, step], ring_recv.at[h, way, step],
-                    place.device(y=sign),
+                    sent[index[h, half, way]].wait_recv()
+                    source = hold.at[h, way, step - 1, half]
+                    source[...] = (
+                        source[...].astype(jnp.float32)
+                        + part_ref[h, target, half].astype(jnp.float32)
+                    ).astype(jnp.bfloat16)
+                copy = ring_copy(
+                    place, source, hold.at[h, way, step, half],
+                    ring_send, ring_recv, h, half, way, step,
                 )
                 copy.start()
-                pending.append(copy)
-                arrived.append(copy)
-            for copy in arrived:
-                copy.wait_recv()
+                index[h, half, way] = len(sent)
+                sent.append(copy)
+
+    def finish(h):
+        for half in range(2):
+            for way in range(2):
+                sent[index[h, half, way]].wait_recv()
         total[h] = (
             part_ref[h, y].astype(jnp.float32)
-            + hold[h, 0, 3].astype(jnp.float32)
-            + hold[h, 1, 3].astype(jnp.float32)
+            + hold[h, 0, HOPS - 1].astype(jnp.float32)
+            + hold[h, 1, HOPS - 1].astype(jnp.float32)
         ).astype(jnp.bfloat16)
-        if h == 1:
-            far = []
-            for m in range(2):
-                far.append(
-                    remote(
-                        total.at[1, (c + m) % 2], grad_ref.at[c, 1],
-                        last_send.at[1 + m], last_recv.at[1 + c], place.device(c=m, z=HALF_Z),
-                    )
-                )
-                far[m].start()
-        else:
-            own = pltpu.make_async_copy(total.at[0, c], grad_ref.at[c, 0], local_sem)
-            own.start()
-            near = remote(
-                total.at[0, 1 - c], grad_ref.at[c, 0],
-                last_send.at[0], last_recv.at[0], place.device(c=1),
-            )
-            near.start()
-    for copy in pending:
+
+    ring(1, 0)
+    ring(1, 1)
+    ring(1, 2)
+    ring(0, 0)
+    ring(1, 3)
+    ring(0, 1)
+    finish(1)
+    legs = far_start(place, total.at[1, c], total.at[1, 1 - c], relay, far_send, far_recv)
+    rows_start(place, rows_ref, home_ref, row_send, row_recv, -1, FIRST_BACK, PEERS)
+    ring(0, 2)
+    ring(0, 3)
+    more = far_relay(
+        place, legs, relay, grad_ref.at[c, 1], grad_ref.at[1 - c, 1], far_send, far_recv
+    )
+    finish(0)
+    own = pltpu.make_async_copy(total.at[0, c], grad_ref.at[c, 0], local_sem)
+    own.start()
+    near = remote(
+        total.at[0, 1 - c], grad_ref.at[c, 0], near_send, near_recv, place.device(c=1)
+    )
+    near.start()
+    for copy in legs + sent:
         copy.wait_send()
     own.wait()
     near.wait()
-    for m in range(2):
-        remote(
-            total.at[1, m], grad_ref.at[m, 1],
-            last_send.at[1 + m], last_recv.at[1 + m], place.device(z=HALF_Z),
-        ).wait()
+    for copy in more:
+        copy.wait()
     rows_wait(place, rows_ref, home_ref, row_send, row_recv, -1)
 
 
@@ -308,8 +333,9 @@
         in_specs=[VMEM] * 2,
         out_specs=(VMEM, VMEM),
         scratch_shapes=[
-            DMA((PEERS,)), DMA((PEERS,)), DMA((3,)), DMA((3,)),
-            DMA((2, 2, 4)), DMA((2, 2, 4)), DMA(()),
+            pltpu.VMEM((2, slice_rows, width), weight_slice.dtype),
+            DMA((PEERS,)), DMA((PEERS,)), DMA((4,)), DMA((4,)), DMA(()), DMA(()),
+            DMA((2, 2, 2, HOPS)), DMA((2, 2, 2, HOPS)), DMA(()),
         ],
         compiler_params=pltpu.CompilerParams(
             collective_id=0, has_side_effects=True, vmem_limit_bytes=VMEM_LIMIT
@@ -329,10 +355,11 @@
         in_specs=[VMEM] * 2,
         out_specs=(VMEM, VMEM),
         scratch_shapes=[
-            pltpu.VMEM((2, 2, 4, 2, slice_rows, width), part.dtype),
+            pltpu.VMEM((2, slice_rows, width), part.dtype),
+            pltpu.VMEM((2, 2, HOPS, 2, slice_rows, width), part.dtype),
             pltpu.VMEM((2, 2, slice_rows, width), part.dtype),
-            DMA((PEERS,)), DMA((PEERS,)), DMA((2, 2, 4)), DMA((2, 2, 4)),
-            DMA((3,)), DMA((3,)), DMA(()),
+            DMA((PEERS,)), DMA((PEERS,)), DMA((4,)), DMA((4,)), DMA(()), DMA(()),
+            DMA((2, 2, 2, HOPS)), DMA((2, 2, 2, HOPS)), DMA(()),
         ],
         compiler_params=pltpu.CompilerParams(
             collective_id=1, has_side_effects=True, vmem_limit_bytes=VMEM_LIMIT
@@ -359,7 +386,7 @@
     here_z = lax.axis_index("grp") % GRID_Z
     core, chip_x, chip_z = slot % members, slot // members // GRID_Z, slot // members % GRID_Z
     d = (chip_z - here_z + GRID_Z) % HALF_Z
-    far = ((here_z + offset_of(d) + GRID_Z) % GRID_Z != chip_z).astype(jnp.int32)
+    far = ((here_z + offset_of(d, core) + GRID_Z) % GRID_Z != chip_z).astype(jnp.int32)
     target = ((core * GRID_X + chip_x) * HALF_Z + d) * block_rows + far * capacity + position
     places = (target[:, None] == lax.iota(jnp.int32, slots)[None, :]).astype(jnp.bfloat16)
     rows = jnp.concatenate([x_rows, y_cot], axis=1)

time: 158 us -> 138 us (0.87)
  the two profiles are of different devices: /device:TPU:1 before, /device:TPU:6 now
where the time goes in v3:
time: 138 us; the launch traced here: 136 us
  Pallas kernels  118 us (86%)
  matrix products  9.43 us (7%)
  other arithmetic  5.03 us (4%)
  local copies, waits for them, and re-layouts  2.94 us (2%)
    pallas_call x1, Pallas kernels, dispatch(): pl.pallas_call(dispatch_kernel, out_shape=(jax.ShapeDtypeStruct(rows.shap...  65.1 us
    pallas_call x1, Pallas kernels, give_back(): pl.pallas_call(return_kernel, out_shape=(jax.ShapeDtypeStruct(rows.shape,...  52.9 us

profile of v3, /device:TPU:6, one launch (start us, length us, event | category | flops | bytes accessed | tf_op | source)
XLA Modules:
  0.0 136.3 jit_solution(6247262057852140897)
XLA Ops:
  0.6 0.7 fusion.18
  1.4 0.6 reduce-window.6
  2.0 0.2 slice_reduce_fusion
  2.3 0.8 select_reduce_fusion
  3.1 2.0 %fusion.rows_ref = bf16[48,8,2432]{2,1,0:T(8,128)(2,1)S(1)} fusion(bf16[256,2048]{1,0:T(8,128)(2,1)} %param.17, bf16[256,384]{1,0:T(8,128)(2,1)} %param.16, s32[256]{0:T(256)S(1)} %fusion.28), kind=kOutput, calls=%fused_computation.2 | convolution fusion | flops 481673216 | bytes 3113984 | tf_op jit(solution)/shard_map/dot_general | solution.py:393
  5.2 65.1 %dispatch.1 = (bf16[48,8,2432]{2,1,0:T(8,128)(2,1)S(1)}, bf16[2,8,2,24,2048]{4,3,2,1,0:T(8,128)(2,1)S(1)}) custom-call(bf16[48,8,2432]{2,1,0:T(8,128)(2,1)S(1)} %fusion.rows_ref, bf16[2,24,2048]{2,1,0:T(8,128)(2,1)S(1)} %convert_element_type.41.slice_ref), custom_call_target="tpu_custom_call" | custom-call | tf_op jit(solution)/shard_map/dispatch/pallas_call | solution.py:327
  70.3 1.4 %fusion.3 = bf16[384,768]{1,0:T(8,128)(2,1)S(1)} fusion(bf16[768,2048]{1,0:T(8,128)(2,1)S(1)} %bitcast.55, bf16[384,2432]{1,0:T(8,128)(2,1)S(1)} %bitcast.52), kind=kOutput, calls=%fused_computation.8 | convolution fusion | flops 1207959552 | bytes 5308416 | tf_op jit(solution)/shard_map/dot_general | solution.py:411
  71.8 0.2 broadcast_select_fusion.1
  72.0 1.4 %convolution_convert_fusion.1 = bf16[48,8,2048]{2,1,0:T(8,128)(2,1)S(1)} fusion(bf16[768,2048,1]{1,0,2:T(8,128)(2,1)S(1)} %bitcast.56, bf16[384,384]{1,0:T(8,128)(2,1)S(1)} %get-tuple-element.29, bf16[384,384]{1,0:T(8,128)(2,1)S(1)} %get-tuple-element.28), kind=kOutput, calls=%fused_computation.3 | convolution fusion | flops 1209925632 | bytes 5308416 | tf_op jit(solution)/shard_map/dot_general | solution.py:410
  73.4 0.2 pad_maximum_fusion.rows_ref
  73.5 1.8 %multiply_convert_fusion = bf16[768,2048]{1,0:T(8,128)(2,1)S(1)} fusion(bf16[384,2432]{1,0:T(8,128)(2,1)S(1)} %bitcast.54, bf16[384,384]{1,0:T(8,128)(2,1)S(1)} %get-tuple-element.29, bf16[384,384]{1,0:T(8,128)(2,1)S(1)} %get-tuple-element.28), kind=kOutput, calls=%fused_computation | convolution fusion | flops 1212284928 | bytes 5308416 | tf_op jit(solution)/shard_map/dot_general | solution.py:404
  75.4 52.9 %give_back.1 = (bf16[48,8,2432]{2,1,0:T(8,128)(2,1)S(1)}, bf16[2,2,24,2048]{3,2,1,0:T(8,128)(2,1)S(1)}) custom-call(bf16[48,8,2432]{2,1,0:T(8,128)(2,1)S(1)} %pad_maximum_fusion.rows_ref, bf16[2,8,2,24,2048]{4,3,2,1,0:T(8,128)(2,1)S(1)} %bitcast.51), custom_call_target="tpu_custom_call" | custom-call | tf_op jit(solution)/shard_map/give_back/pallas_call | solution.py:349
  128.2 1.7 %convolution_convert_fusion.2 = bf16[256,2048]{1,0:T(8,128)(2,1)} fusion(bf16[384,2432]{1,0:T(8,128)(2,1)S(1)} %bitcast.57, s32[256]{0:T(256)S(1)} %fusion.28), kind=kOutput, calls=%fused_computation.4 | convolution fusion | flops 403275776 | bytes 2622464 | tf_op jit(solution)/shard_map/dot_general | solution.py:418
  130.0 1.0 convolution_convert_fusion.3
  131.1 0.1 copy.26
  131.2 0.2 mul.99
  131.4 0.1 fusion.32
  131.5 0.2 copy-done.4
  131.7 0.1 copy.27
  131.8 0.2 mul.106
  132.0 0.1 mul.107
  132.0 0.1 copy.31
  132.1 0.2 bitcast_reduce_fusion.1
  132.3 0.2 div.94
  132.5 0.1 div.95
  132.6 1.1 multiply_subtract_fusion
  133.7 0.7 copy.28
  134.3 0.1 copy.32
  134.4 0.2 bitcast_reduce_fusion
  134.6 0.2 div.97
  134.8 0.7 divide_convert_fusion
  135.6 0.7 copy.29
  (19 shorter events, 0.3 us)
Async XLA Ops:
  0.6 4.6 %copy-start = (f32[2,24,2048]{2,1,0:T(8,128)S(1)}, f32[2,24,2048]{2,1,0:T(8,128)}, u32[]{:S(2)}) copy-start(f32[2,24,2048]{2,1,0:T(8,128)} %param.9) | copy-start | bytes 1179652
  128.2 2.8 %copy-start.3 = (f32[2,24,16]{1,2,0:T(8,128)S(1)}, f32[2,24,16]{1,2,0:T(8,128)}, u32[]{:S(2)}) copy-start(f32[2,24,16]{1,2,0:T(8,128)} %param.11) | copy-start | bytes 9220
  130.0 1.4 %copy-start.1 = (bf16[2,24,2048]{2,1,0:T(8,128)(2,1)S(1)}, bf16[2,24,2048]{2,1,0:T(8,128)(2,1)}, u32[]{:S(2)}) copy-start(bf16[2,24,2048]{2,1,0:T(8,128)(2,1)} %param.10) | copy-start | bytes 589828
  131.0 0.7 copy-start.4
  131.5 1.0 copy-start.2

commit v4 on v3

--- a/solution.py
+++ b/solution.py
@@ -17,6 +17,7 @@
 FIRST_ROWS = 4
 FIRST_BACK = 24
 VMEM_LIMIT = 40 * 1024 * 1024
+FIRST_LIMIT = VMEM_LIMIT
 
 
 beta_one = 0.9
@@ -24,24 +25,57 @@
 learn_rate = 0.01
 
 
-def adam_update(master_weight, grad, m_code, m_scale, v_code, v_scale):
-    full_shape = master_weight.shape
-    blocked = full_shape[:-1] + (full_shape[-1] // BLOCK, BLOCK)
-    m_old = (m_code.astype(jnp.float32).reshape(blocked) * m_scale[..., None]).reshape(full_shape)
-    v_old = (v_code.astype(jnp.float32).reshape(blocked) * v_scale[..., None]).reshape(full_shape)
-    m_next = beta_one * m_old + (1.0 - beta_one) * grad
-    v_next = beta_two * v_old + (1.0 - beta_two) * grad * grad
+def adam_kernel(
+    weight_ref, m_code_ref, m_scale_ref, v_code_ref, v_scale_ref, grad_ref,
+    weight_out, m_code_out, m_scale_out, v_code_out, v_scale_out,
+):
+    members, rows, width = weight_ref.shape
+    i = lax.broadcasted_iota(jnp.int32, (rows, rows), 0)
+    j = lax.broadcasted_iota(jnp.int32, (rows, rows), 1)
     corr_one = 1.0 - beta_one**ADAM_STEP
     corr_two = 1.0 - beta_two**ADAM_STEP
-    step_size = m_next / corr_one / (jnp.sqrt(v_next / corr_two) + 1e-08)
-    master_next = master_weight - learn_rate * step_size
-    m_blocks = m_next.reshape(blocked)
-    v_blocks = v_next.reshape(blocked)
-    m_scale_next = jnp.max(jnp.abs(m_blocks), axis=-1) + 1e-06
-    v_scale_next = jnp.max(v_blocks, axis=-1) + 1e-06
-    m_code_next = (m_blocks / m_scale_next[..., None]).reshape(full_shape).astype(jnp.bfloat16)
-    v_code_next = (v_blocks / v_scale_next[..., None]).reshape(full_shape).astype(jnp.bfloat16)
-    return (master_next, m_code_next, m_scale_next, v_code_next, v_scale_next)
+
+    def load_scale(ref, e, b):
+        return jnp.sum(jnp.where(i == j, ref[e, b : b + 1, :], 0.0), axis=1, keepdims=True)
+
+    def store_scale(ref, e, b, value):
+        ref[e, b : b + 1, :] = jnp.sum(jnp.where(i == j, value, 0.0), axis=0, keepdims=True)
+
+    for e in range(members):
+        for b in range(width // BLOCK):
+            at = slice(b * BLOCK, (b + 1) * BLOCK)
+            grad = grad_ref[e, 0, :, at].astype(jnp.float32) + grad_ref[e, 1, :, at].astype(
+                jnp.float32
+            )
+            m_old = m_code_ref[e, :, at].astype(jnp.float32) * load_scale(m_scale_ref, e, b)
+            v_old = v_code_ref[e, :, at].astype(jnp.float32) * load_scale(v_scale_ref, e, b)
+            m_next = beta_one * m_old + (1.0 - beta_one) * grad
+            v_next = beta_two * v_old + (1.0 - beta_two) * grad * grad
+            step_size = m_next / corr_one / (jnp.sqrt(v_next / corr_two) + 1e-08)
+            weight_out[e, :, at] = weight_ref[e, :, at] - learn_rate * step_size
+            m_scale_next = jnp.max(jnp.abs(m_next), axis=-1, keepdims=True) + 1e-06
+            v_scale_next = jnp.max(v_next, axis=-1, keepdims=True) + 1e-06
+            m_code_out[e, :, at] = (m_next / m_scale_next).astype(jnp.bfloat16)
+            v_code_out[e, :, at] = (v_next / v_scale_next).astype(jnp.bfloat16)
+            store_scale(m_scale_out, e, b, m_scale_next)
+            store_scale(v_scale_out, e, b, v_scale_next)
+
+
+def adam_update(master_weight, grad_pairs, m_code, m_scale, v_code, v_scale):
+    turned = [jnp.swapaxes(scale, 1, 2) for scale in (m_scale, v_scale)]
+    like = [
+        jax.ShapeDtypeStruct(array.shape, array.dtype)
+        for array in (master_weight, m_code, turned[0], v_code, turned[1])
+    ]
+    weight, m_next, m_rows, v_next, v_rows = pl.pallas_call(
+        adam_kernel,
+        out_shape=like,
+        in_specs=[pl.BlockSpec(memory_space=pltpu.VMEM)] * 6,
+        out_specs=[pl.BlockSpec(memory_space=pltpu.VMEM)] * 5,
+        compiler_params=pltpu.CompilerParams(vmem_limit_bytes=VMEM_LIMIT // 2),
+        name="adam",
+    )(master_weight, m_code, turned[0], v_code, turned[1], grad_pairs)
+    return (weight, m_next, jnp.swapaxes(m_rows, 1, 2), v_next, jnp.swapaxes(v_rows, 1, 2))
 
 
 def offset_of(d, member):
@@ -75,7 +109,7 @@
     return c, x, d
 
 
-def enter(place, sign):
+def greet_all(place, sign):
     def greet(i, carry):
         c, x, d = peer(i)
         member = place.c if sign == 1 else (place.c + c) % 2
@@ -92,7 +126,42 @@
     signal(place.device(y=1))
     signal(place.device(y=-1))
     lax.fori_loop(0, PEERS, greet, 0)
+
+
+def wait_all():
     pl.semaphore_wait(pltpu.get_barrier_semaphore(), PEERS - 1 + 5)
+
+
+def column(row):
+    size = row.shape[1]
+    i = lax.broadcasted_iota(jnp.int32, (size, size), 0)
+    j = lax.broadcasted_iota(jnp.int32, (size, size), 1)
+    return jnp.sum(jnp.where(i == j, row, 0.0), axis=1, keepdims=True)
+
+
+def targets(place, placement, route):
+    experts, rows = placement.shape[1], route.shape[1]
+    route = route.astype(jnp.float32)
+    i = lax.broadcasted_iota(jnp.int32, (rows, rows), 0)
+    j = lax.broadcasted_iota(jnp.int32, (rows, rows), 1)
+    earlier = jnp.logical_and(column(route) == route, i < j)
+    position = jnp.sum(jnp.where(earlier, 1.0, 0.0), axis=0, keepdims=True).astype(jnp.int32)
+    ids = lax.broadcasted_iota(jnp.int32, (experts, rows), 0).astype(jnp.float32)
+    hit = column(placement.astype(jnp.float32)) == route
+    slot = jnp.sum(jnp.where(hit, ids, 0.0), axis=0, keepdims=True).astype(jnp.int32)
+
+    def count(value, step, most):
+        return sum(jnp.where(value >= k * step, 1, 0) for k in range(1, most))
+
+    core, group = slot & 1, slot >> 1
+    chip_x = count(group, GRID_Z, GRID_X)
+    chip_z = group - GRID_Z * chip_x
+    ahead = chip_z - place.z + GRID_Z
+    d = ahead - HALF_Z * count(ahead, HALF_Z, 4)
+    delta = place.z + offset_of(d, core) - chip_z
+    near = jnp.logical_or(delta == 0, jnp.logical_or(delta == GRID_Z, delta == -GRID_Z))
+    far = jnp.where(near, 0, 1)
+    return ((core * GRID_X + chip_x) * HALF_Z + d) * 8 + far * 4 + position
 
 
 def rows_start(place, source, target, send_sem, recv_sem, sign, low, high):
@@ -187,13 +256,43 @@
 
 
 def dispatch_kernel(
-    rows_ref, slice_ref, recv_ref, full_ref,
-    relay, row_send, row_recv, far_send, far_recv, near_send, near_recv,
+    placement_ref, route_ref, x_hbm, g_hbm, weight_hbm, recv_ref, full_ref, target_ref,
+    x_ref, g_ref, weight_ref, rows_ref, slice_ref, load_sem, relay, row_send, row_recv, far_send, far_recv, near_send, near_recv,
     ring_send, ring_recv, local_sem,
 ):
     place = Place()
     y, c = place.y, place.c
-    enter(place, 1)
+    loads = [
+        pltpu.make_async_copy(source, into, load_sem.at[i])
+        for i, (source, into) in enumerate(
+            ((weight_hbm, weight_ref), (x_hbm, x_ref), (g_hbm, g_ref))
+        )
+    ]
+    for load in loads:
+        load.start()
+    greet_all(place, 1)
+    target = targets(place, placement_ref[...], route_ref[...])
+    target_ref[...] = target
+    slots, row_count = PEERS * 8, x_ref.shape[0]
+    places = lax.broadcasted_iota(jnp.int32, (slots, row_count), 0) == target
+    places = jnp.where(places, 1.0, 0.0).astype(jnp.bfloat16)
+    loads[0].wait()
+    slice_ref[...] = weight_ref[...].astype(jnp.bfloat16)
+    loads[1].wait()
+    hidden = x_ref.shape[1]
+    rows_ref[:, :, :hidden] = (
+        jnp.dot(places, x_ref[...], preferred_element_type=jnp.float32)
+        .reshape(PEERS, 8, hidden)
+        .astype(jnp.bfloat16)
+    )
+    loads[2].wait()
+    for j in range(0, g_ref.shape[1], 512):
+        rows_ref[:, :, hidden + j : hidden + j + 512] = (
+            jnp.dot(places, g_ref[:, j : j + 512], preferred_element_type=jnp.float32)
+            .reshape(PEERS, 8, 512)
+            .astype(jnp.bfloat16)
+        )
+    wait_all()
     own = pltpu.make_async_copy(slice_ref.at[c], full_ref.at[0, y, c], local_sem)
     own.start()
     near = remote(
@@ -249,7 +348,8 @@
 ):
     place = Place()
     y, c = place.y, place.c
-    enter(place, -1)
+    greet_all(place, -1)
+    wait_all()
     rows_start(place, rows_ref, home_ref, row_send, row_recv, -1, 0, FIRST_BACK)
     sent = []
     index = {}
@@ -322,26 +422,43 @@
 DMA = pltpu.SemaphoreType.DMA
 
 
-def dispatch(rows, weight_slice):
-    members, slice_rows, width = weight_slice.shape
+def dispatch(placement, route, x_rows, y_cot, master_weight):
+    members, slice_rows, width = master_weight.shape
+    row_count, hidden = x_rows.shape
+    hbm = pl.BlockSpec(memory_space=pltpu.HBM)
+    low = jnp.bfloat16
     return pl.pallas_call(
         dispatch_kernel,
         out_shape=(
-            jax.ShapeDtypeStruct(rows.shape, rows.dtype),
-            jax.ShapeDtypeStruct((2, GRID_Y, 2, slice_rows, width), weight_slice.dtype),
+            jax.ShapeDtypeStruct((PEERS, 8, hidden + width), low),
+            jax.ShapeDtypeStruct((2, GRID_Y, 2, slice_rows, width), low),
+            jax.ShapeDtypeStruct((1, row_count), jnp.int32),
         ),
-        in_specs=[VMEM] * 2,
-        out_specs=(VMEM, VMEM),
+        in_specs=[VMEM, VMEM, hbm, hbm, hbm],
+        out_specs=(VMEM, VMEM, VMEM),
         scratch_shapes=[
-            pltpu.VMEM((2, slice_rows, width), weight_slice.dtype),
+            pltpu.VMEM(x_rows.shape, low),
+            pltpu.VMEM(y_cot.shape, low),
+            pltpu.VMEM(master_weight.shape, jnp.float32),
+            pltpu.VMEM((PEERS, 8, hidden + width), low),
+            pltpu.VMEM(master_weight.shape, low),
+            DMA((3,)),
+            pltpu.VMEM((2, slice_rows, width), low),
             DMA((PEERS,)), DMA((PEERS,)), DMA((4,)), DMA((4,)), DMA(()), DMA(()),
             DMA((2, 2, 2, HOPS)), DMA((2, 2, 2, HOPS)), DMA(()),
         ],
         compiler_params=pltpu.CompilerParams(
-            collective_id=0, has_side_effects=True, vmem_limit_bytes=VMEM_LIMIT
+            collective_id=0, has_side_effects=True, vmem_limit_bytes=FIRST_LIMIT
         ),
         name="dispatch",
-    )(rows, weight_slice)
+    )(
+        *(
+            pltpu.with_memory_space_constraint(array, pltpu.HBM)
+            for array in (
+                placement.reshape(1, -1), route.reshape(1, -1), x_rows, y_cot, master_weight
+            )
+        )
+    )
 
 
 def give_back(rows, part):
@@ -378,23 +495,9 @@
     capacity = max(2, (3 * row_count + 2 * expert_count - 1) // (2 * expert_count))
     block_rows = 2 * capacity
     slots = PEERS * block_rows
-    weight_slice = master_weight.astype(jnp.bfloat16)
-    expert_ids = lax.iota(jnp.int32, expert_count)
-    route_hot = (route[:, None] == expert_ids[None, :]).astype(jnp.int32)
-    position = jnp.sum(route_hot * (jnp.cumsum(route_hot, axis=0) - 1), axis=1)
-    slot = jnp.sum(jnp.where(placement[None, :] == route[:, None], expert_ids[None, :], 0), axis=1)
-    here_z = lax.axis_index("grp") % GRID_Z
-    core, chip_x, chip_z = slot % members, slot // members // GRID_Z, slot // members % GRID_Z
-    d = (chip_z - here_z + GRID_Z) % HALF_Z
-    far = ((here_z + offset_of(d, core) + GRID_Z) % GRID_Z != chip_z).astype(jnp.int32)
-    target = ((core * GRID_X + chip_x) * HALF_Z + d) * block_rows + far * capacity + position
-    places = (target[:, None] == lax.iota(jnp.int32, slots)[None, :]).astype(jnp.bfloat16)
-    rows = jnp.concatenate([x_rows, y_cot], axis=1)
-    send = lax.dot_general(
-        places, rows, (((0,), (0,)), ((), ())), preferred_element_type=jnp.float32
-    ).astype(jnp.bfloat16)
     width = hidden_width + model_width
-    recv, full = dispatch(send.reshape(PEERS, block_rows, width), weight_slice)
+    recv, full, target = dispatch(placement, route, x_rows, y_cot, master_weight)
+    places = (target.reshape(-1, 1) == lax.iota(jnp.int32, slots)[None, :]).astype(jnp.bfloat16)
     recv = recv.reshape(slots, width)
     half = lax.broadcasted_iota(jnp.int32, (slots, 1), 0) % block_rows // capacity
     local_x, local_g = recv[:, :hidden_width], recv[:, hidden_width:]
@@ -421,8 +524,7 @@
     x_grad = jnp.dot(places, home[:, :hidden_width], preferred_element_type=jnp.float32).astype(
         jnp.bfloat16
     )
-    grad = jnp.sum(grad_pairs.astype(jnp.float32), axis=1)
-    return (y_rows, x_grad) + adam_update(master_weight, grad, m_code, m_scale, v_code, v_scale)
+    return (y_rows, x_grad) + adam_update(master_weight, grad_pairs, m_code, m_scale, v_code, v_scale)
 
 
 def solution(mesh):

time: 138 us -> 133 us (0.964)
  Pallas kernels: 118 us -> 123 us
  other arithmetic: 5.03 us -> 0.38 us
  local copies, waits for them, and re-layouts: 2.94 us -> 0.03 us
  matrix products: 9.43 us -> 7.43 us
    pallas_call x1 -> x2, Pallas kernels: 65.1 us -> 68 us  [the longest x1 65.3 us: dispatch(): pl.pallas_call(dispatch_kernel, out_shape=(jax.ShapeDtypeStruct((PEERS, 8...]
    pallas_call x1, Pallas kernels: 52.9 us -> 55 us  [give_back(): pl.pallas_call(return_kernel, out_shape=(jax.ShapeDtypeStruct(rows.shape,...]
    dot_general x1 -> x0, matrix products: 2.03 us -> none  [per_device(): lax.dot_general(places, rows, (((0,), (0,)), ((), ())), preferred_element...]
    unnamed x16 -> x10, local copies, waits for them, and re-layouts: 1.87 us -> 0.03 us
    convert_element_type x3 -> x0, other arithmetic: 1.5 us -> none  [the longest x1 0.74 us: per_device(): route_hot = (route[:, None] == expert_ids[None, :]).astype(jnp.int32)]
where the time goes in v4:
time: 133 us; the launch traced here: 132 us
  Pallas kernels  123 us (92%)
  matrix products  7.43 us (6%)
    pallas_call x1, Pallas kernels, dispatch(): pl.pallas_call(dispatch_kernel, out_shape=(jax.ShapeDtypeStruct((PEERS, 8...  65.3 us
    pallas_call x1, Pallas kernels, give_back(): pl.pallas_call(return_kernel, out_shape=(jax.ShapeDtypeStruct(rows.shape,...  55 us
    pallas_call x1, Pallas kernels, adam_update(): pl.pallas_call(adam_kernel, out_shape=like, in_specs=[pl.BlockSpec(memory...  2.74 us

profile of v4, /device:TPU:6, one launch (start us, length us, event | category | flops | bytes accessed | tf_op | source)
XLA Modules:
  0.0 131.6 jit_solution(7293030800997777750)
XLA Ops:
  0.6 65.3 %dispatch.1 = (bf16[48,8,2432]{2,1,0:T(8,128)(2,1)S(1)}, bf16[2,8,2,24,2048]{4,3,2,1,0:T(8,128)(2,1)S(1)}, s32[1,256]{1,0:T(1,128)S(1)}) custom-call(s32[1,96]{1,0:T(1,128)} %bitcast.33, s32[1,256]{1,0:T(1,128)} %bitcast.32, bf16[256,384]{1,0:T(8,128)(2,1)} %x_hbm.1, bf16[256,2048]{1,0:T(8,128)(2,1)} %g_hbm.1, f32[2,24,2048]{2,1,0:T(8,128)} %weight_ref.1), custom_call_target="tpu_custom_call" | custom-call | tf_op jit(solution)/shard_map/dispatch/pallas_call | solution.py:430
  66.0 1.5 %fusion.2 = bf16[384,768]{1,0:T(8,128)(2,1)S(1)} fusion(bf16[768,2048]{1,0:T(8,128)(2,1)S(1)} %bitcast.26, bf16[384,2432]{1,0:T(8,128)(2,1)S(1)} %bitcast.21), kind=kOutput, calls=%fused_computation.6 | convolution fusion | flops 1207959552 | bytes 5308416 | tf_op jit(solution)/shard_map/dot_general | solution.py:514
  67.4 0.2 broadcast_select_fusion.1
  67.6 1.4 %convolution_convert_fusion = bf16[48,8,2048]{2,1,0:T(8,128)(2,1)S(1)} fusion(bf16[768,2048,1]{1,0,2:T(8,128)(2,1)S(1)} %bitcast.27, bf16[384,384]{1,0:T(8,128)(2,1)S(1)} %get-tuple-element.28, bf16[384,384]{1,0:T(8,128)(2,1)S(1)} %get-tuple-element.27), kind=kOutput, calls=%fused_computation.1 | convolution fusion | flops 1209925632 | bytes 5308416 | tf_op jit(solution)/shard_map/dot_general | solution.py:513
  69.0 0.2 pad_maximum_fusion.rows_ref
  69.2 1.8 %multiply_convert_fusion = bf16[768,2048]{1,0:T(8,128)(2,1)S(1)} fusion(bf16[384,2432]{1,0:T(8,128)(2,1)S(1)} %bitcast.23, bf16[384,384]{1,0:T(8,128)(2,1)S(1)} %get-tuple-element.28, bf16[384,384]{1,0:T(8,128)(2,1)S(1)} %get-tuple-element.27), kind=kOutput, calls=%fused_computation | convolution fusion | flops 1212284928 | bytes 5308416 | tf_op jit(solution)/shard_map/dot_general | solution.py:507
  71.0 55.0 %give_back.1 = (bf16[48,8,2432]{2,1,0:T(8,128)(2,1)S(1)}, bf16[2,2,24,2048]{3,2,1,0:T(8,128)(2,1)S(1)}) custom-call(bf16[48,8,2432]{2,1,0:T(8,128)(2,1)S(1)} %pad_maximum_fusion.rows_ref, bf16[2,8,2,24,2048]{4,3,2,1,0:T(8,128)(2,1)S(1)} %bitcast.20), custom_call_target="tpu_custom_call" | custom-call | tf_op jit(solution)/shard_map/give_back/pallas_call | solution.py:466
  126.0 0.0 copy-start
  126.1 0.0 copy-start.1
  126.1 0.0 copy-start.2
  126.1 0.0 copy-start.3
  126.1 0.0 copy-start.4
  126.1 1.0 convolution_convert_fusion.2
  127.1 1.7 %convolution_convert_fusion.1 = bf16[256,2048]{1,0:T(8,128)(2,1)} fusion(bf16[384,2432]{1,0:T(8,128)(2,1)S(1)} %bitcast.29, s32[256]{0:T(256)S(1)} %bitcast.31), kind=kOutput, calls=%fused_computation.2 | convolution fusion | flops 403275776 | bytes 2622464 | tf_op jit(solution)/shard_map/dot_general | solution.py:521
  128.9 0.0 copy-done
  128.9 0.0 copy-done.1
  128.9 0.0 copy-done.2
  128.9 0.0 copy-done.3
  128.9 0.0 copy-done.4
  128.9 2.7 %adam.1 = (f32[2,24,2048]{2,1,0:T(8,128)}, bf16[2,24,2048]{2,1,0:T(8,128)(2,1)}, f32[2,16,24]{2,1,0:T(8,128)}, bf16[2,24,2048]{2,1,0:T(8,128)(2,1)}, f32[2,16,24]{2,1,0:T(8,128)}) custom-call(f32[2,24,2048]{2,1,0:T(8,128)S(1)} %copy-done, bf16[2,24,2048]{2,1,0:T(8,128)(2,1)S(1)} %copy-done.1, f32[2,16,24]{2,1,0:T(8,128)S(1)} %bitcast.24, ...), custom_call_target="tpu_custom_call" | custom-call | tf_op jit(solution)/shard_map/adam/pallas_call | solution.py:70
  (1 shorter events, 0.0 us)
Async XLA Ops:
  126.0 2.8 %copy-start = (f32[2,24,2048]{2,1,0:T(8,128)S(1)}, f32[2,24,2048]{2,1,0:T(8,128)}, u32[]{:S(2)}) copy-start(f32[2,24,2048]{2,1,0:T(8,128)} %weight_ref.1) | copy-start | bytes 1179652
  126.1 2.8 %copy-start.1 = (bf16[2,24,2048]{2,1,0:T(8,128)(2,1)S(1)}, bf16[2,24,2048]{2,1,0:T(8,128)(2,1)}, u32[]{:S(2)}) copy-start(bf16[2,24,2048]{2,1,0:T(8,128)(2,1)} %m_code_ref.1) | copy-start | bytes 589828
  126.1 2.8 %copy-start.2 = (bf16[2,24,2048]{2,1,0:T(8,128)(2,1)S(1)}, bf16[2,24,2048]{2,1,0:T(8,128)(2,1)}, u32[]{:S(2)}) copy-start(bf16[2,24,2048]{2,1,0:T(8,128)(2,1)} %v_code_ref.1) | copy-start | bytes 589828
  126.1 2.8 %copy-start.3 = (f32[2,24,16]{1,2,0:T(8,128)S(1)}, f32[2,24,16]{1,2,0:T(8,128)}, u32[]{:S(2)}) copy-start(f32[2,24,16]{1,2,0:T(8,128)} %param.11) | copy-start | bytes 9220
  126.1 2.8 %copy-start.4 = (f32[2,24,16]{1,2,0:T(8,128)S(1)}, f32[2,24,16]{1,2,0:T(8,128)}, u32[]{:S(2)}) copy-start(f32[2,24,16]{1,2,0:T(8,128)} %param.13) | copy-start | bytes 9220

commit v5 on v4

--- a/solution.py
+++ b/solution.py
@@ -14,7 +14,7 @@
 PEERS = 2 * GRID_X * HALF_Z
 MESH = pl.DeviceIdType.MESH
 HOPS = 4
-FIRST_ROWS = 4
+FIRST_ROWS = 2
 FIRST_BACK = 24
 VMEM_LIMIT = 40 * 1024 * 1024
 FIRST_LIMIT = VMEM_LIMIT

time: 133 us -> 132 us (level); the launches traced: 132 us -> 132 us
  no operation moved by 1% of the time
where the time goes in v5:
time: 132 us
  Pallas kernels  124 us (94%)
  matrix products  7.43 us (6%)
    pallas_call x1, Pallas kernels, dispatch(): pl.pallas_call(dispatch_kernel, out_shape=(jax.ShapeDtypeStruct((PEERS, 8...  66 us
    pallas_call x1, Pallas kernels, give_back(): pl.pallas_call(return_kernel, out_shape=(jax.ShapeDtypeStruct(rows.shape,...  54.8 us
    pallas_call x1, Pallas kernels, adam_update(): pl.pallas_call(adam_kernel, out_shape=like, in_specs=[pl.BlockSpec(memory...  2.74 us

profile of v5, /device:TPU:6, one launch (start us, length us, event | category | flops | bytes accessed | tf_op | source)
XLA Modules:
  0.0 132.1 jit_solution(7714257497828197375)
XLA Ops:
  0.6 66.0 %dispatch.1 = (bf16[48,8,2432]{2,1,0:T(8,128)(2,1)S(1)}, bf16[2,8,2,24,2048]{4,3,2,1,0:T(8,128)(2,1)S(1)}, s32[1,256]{1,0:T(1,128)S(1)}) custom-call(s32[1,96]{1,0:T(1,128)} %bitcast.33, s32[1,256]{1,0:T(1,128)} %bitcast.32, bf16[256,384]{1,0:T(8,128)(2,1)} %x_hbm.1, bf16[256,2048]{1,0:T(8,128)(2,1)} %g_hbm.1, f32[2,24,2048]{2,1,0:T(8,128)} %weight_ref.1), custom_call_target="tpu_custom_call" | custom-call | tf_op jit(solution)/shard_map/dispatch/pallas_call | solution.py:430
  66.6 1.5 %fusion.2 = bf16[384,768]{1,0:T(8,128)(2,1)S(1)} fusion(bf16[768,2048]{1,0:T(8,128)(2,1)S(1)} %bitcast.26, bf16[384,2432]{1,0:T(8,128)(2,1)S(1)} %bitcast.21), kind=kOutput, calls=%fused_computation.6 | convolution fusion | flops 1207959552 | bytes 5308416 | tf_op jit(solution)/shard_map/dot_general | solution.py:514
  68.1 0.2 broadcast_select_fusion.1
  68.3 1.4 %convolution_convert_fusion = bf16[48,8,2048]{2,1,0:T(8,128)(2,1)S(1)} fusion(bf16[768,2048,1]{1,0,2:T(8,128)(2,1)S(1)} %bitcast.27, bf16[384,384]{1,0:T(8,128)(2,1)S(1)} %get-tuple-element.28, bf16[384,384]{1,0:T(8,128)(2,1)S(1)} %get-tuple-element.27), kind=kOutput, calls=%fused_computation.1 | convolution fusion | flops 1209925632 | bytes 5308416 | tf_op jit(solution)/shard_map/dot_general | solution.py:513
  69.7 0.2 pad_maximum_fusion.rows_ref
  69.9 1.8 %multiply_convert_fusion = bf16[768,2048]{1,0:T(8,128)(2,1)S(1)} fusion(bf16[384,2432]{1,0:T(8,128)(2,1)S(1)} %bitcast.23, bf16[384,384]{1,0:T(8,128)(2,1)S(1)} %get-tuple-element.28, bf16[384,384]{1,0:T(8,128)(2,1)S(1)} %get-tuple-element.27), kind=kOutput, calls=%fused_computation | convolution fusion | flops 1212284928 | bytes 5308416 | tf_op jit(solution)/shard_map/dot_general | solution.py:507
  71.7 54.8 %give_back.1 = (bf16[48,8,2432]{2,1,0:T(8,128)(2,1)S(1)}, bf16[2,2,24,2048]{3,2,1,0:T(8,128)(2,1)S(1)}) custom-call(bf16[48,8,2432]{2,1,0:T(8,128)(2,1)S(1)} %pad_maximum_fusion.rows_ref, bf16[2,8,2,24,2048]{4,3,2,1,0:T(8,128)(2,1)S(1)} %bitcast.20), custom_call_target="tpu_custom_call" | custom-call | tf_op jit(solution)/shard_map/give_back/pallas_call | solution.py:466
  126.5 0.0 copy-start
  126.6 0.0 copy-start.1
  126.6 0.0 copy-start.2
  126.6 0.0 copy-start.3
  126.6 0.0 copy-start.4
  126.6 1.0 convolution_convert_fusion.2
  127.6 1.7 %convolution_convert_fusion.1 = bf16[256,2048]{1,0:T(8,128)(2,1)} fusion(bf16[384,2432]{1,0:T(8,128)(2,1)S(1)} %bitcast.29, s32[256]{0:T(256)S(1)} %bitcast.31), kind=kOutput, calls=%fused_computation.2 | convolution fusion | flops 403275776 | bytes 2622464 | tf_op jit(solution)/shard_map/dot_general | solution.py:521
  129.4 0.0 copy-done
  129.4 0.0 copy-done.1
  129.4 0.0 copy-done.2
  129.4 0.0 copy-done.3
  129.4 0.0 copy-done.4
  129.4 2.7 %adam.1 = (f32[2,24,2048]{2,1,0:T(8,128)}, bf16[2,24,2048]{2,1,0:T(8,128)(2,1)}, f32[2,16,24]{2,1,0:T(8,128)}, bf16[2,24,2048]{2,1,0:T(8,128)(2,1)}, f32[2,16,24]{2,1,0:T(8,128)}) custom-call(f32[2,24,2048]{2,1,0:T(8,128)S(1)} %copy-done, bf16[2,24,2048]{2,1,0:T(8,128)(2,1)S(1)} %copy-done.1, f32[2,16,24]{2,1,0:T(8,128)S(1)} %bitcast.24, ...), custom_call_target="tpu_custom_call" | custom-call | tf_op jit(solution)/shard_map/adam/pallas_call | solution.py:70
  (1 shorter events, 0.0 us)
Async XLA Ops:
  126.5 2.8 %copy-start = (f32[2,24,2048]{2,1,0:T(8,128)S(1)}, f32[2,24,2048]{2,1,0:T(8,128)}, u32[]{:S(2)}) copy-start(f32[2,24,2048]{2,1,0:T(8,128)} %weight_ref.1) | copy-start | bytes 1179652
  126.6 2.8 %copy-start.1 = (bf16[2,24,2048]{2,1,0:T(8,128)(2,1)S(1)}, bf16[2,24,2048]{2,1,0:T(8,128)(2,1)}, u32[]{:S(2)}) copy-start(bf16[2,24,2048]{2,1,0:T(8,128)(2,1)} %m_code_ref.1) | copy-start | bytes 589828
  126.6 2.8 %copy-start.2 = (bf16[2,24,2048]{2,1,0:T(8,128)(2,1)S(1)}, bf16[2,24,2048]{2,1,0:T(8,128)(2,1)}, u32[]{:S(2)}) copy-start(bf16[2,24,2048]{2,1,0:T(8,128)(2,1)} %v_code_ref.1) | copy-start | bytes 589828
  126.6 2.8 %copy-start.3 = (f32[2,24,16]{1,2,0:T(8,128)S(1)}, f32[2,24,16]{1,2,0:T(8,128)}, u32[]{:S(2)}) copy-start(f32[2,24,16]{1,2,0:T(8,128)} %param.11) | copy-start | bytes 9220
  126.6 2.8 %copy-start.4 = (f32[2,24,16]{1,2,0:T(8,128)S(1)}, f32[2,24,16]{1,2,0:T(8,128)}, u32[]{:S(2)}) copy-start(f32[2,24,16]{1,2,0:T(8,128)} %param.13) | copy-start | bytes 9220
